TPU v7x, 256 devices: a whole 4x4x8 slice. The times are simulated.
256 devices in a mesh: gx: 16 (over y, x_lo, core), yz: 16 (over z, x_hi).
Axes of the slice: x: 4 (x_hi: 2, x_lo: 2; x = x_hi * 2 + x_lo), y: 4, z: 8, core: 2. Of those that a mesh axis runs over, the one named last changes fastest.
Arguments:
- a_blocks: bfloat16 [4096, 64, 448], P(('gx', 'yz')), may hold values from -0.75 to 0.75
- p_blocks: bfloat16 [4096, 64, 192], P(('gx', 'yz')), may hold values from -0.75 to 0.75
- a_slot: int32 [4096, 7], P(('gx', 'yz')), may hold values from 0 to 31
- halo_rows: int32 [256, 4, 4], P(('gx', 'yz')), may hold values from 0 to 15
- p_cols: int32 [4096, 3], P(('gx', 'yz')), may hold values from 0 to 8, as said below
- t_slot: int32 [4096, 3, 7, 3], P(('gx', 'yz')), may hold values from 0 to 8
Outputs:
- coarse: float32 [512, 64, 576], P(('gx', 'yz'))
Inputs may be any that keep to these rules, and one draw needn't show every extreme that they name: `a_slot`: values below 16 name the device's own element rows; a value v of 16 or more names entry (v - 16) % 4 of the list for neighbour (v - 16) // 4. `halo_rows`: entry [d, k, h] is a local row index on the k-th neighbour of device d. `p_cols`: value r names local aggregate r % 2 of the device itself if r // 2 = 0, else local aggregate r % 2 of its neighbour number r // 2 - 1, and then r % 2 is below 1.
All inputs are finite; a program needn't handle non-finite values.
Results may differ from a plain program's by a relative error of at most 0.004.
Values may be sent and summed in bfloat16 or wider, within the bound.
No kernel may reach another device: no remote copies, remote signals or barrier semaphores. Data moves between devices by JAX's collectives and lax.ppermute only.
A program may use at most 128 MiB of HBM per device.

v0:
```python
import jax
import jax.numpy as jnp
from jax import lax
from jax.sharding import PartitionSpec as P

KC = 9


def shifted(value, axis, steps):
    count = lax.axis_size(axis)
    pairs = [(source, (source + steps) % count) for source in range(count)]
    return lax.ppermute(value, axis, pairs)


def shards(a_blocks, p_blocks, a_slot, halo_rows, p_cols, t_slot):
    elements = a_blocks.shape[0]
    block = a_blocks.shape[1]
    count_a = a_blocks.shape[2] // block
    count_p = p_cols.shape[1]
    coarse_width = p_blocks.shape[2] // count_p
    slot_count = KC
    row_width = slot_count * coarse_width
    aggregates = elements // 8
    boundary = max(aggregates // 4, 1)
    wanted = halo_rows[0]
    pieces = []
    for offset in (1, -1):
        whole = shifted(p_blocks, "gx", offset)
        pieces.append(jnp.take(whole, wanted[0 if offset == 1 else 1], axis=0))
    for offset in (1, -1):
        whole = shifted(p_blocks, "yz", offset)
        pieces.append(jnp.take(whole, wanted[2 if offset == 1 else 3], axis=0))
    extended = jnp.concatenate([p_blocks] + pieces, axis=0)
    fetched = jnp.take(extended, a_slot, axis=0)
    a_split = a_blocks.reshape(elements, block, count_a, block)
    product = jnp.einsum(
        "ixay,iayn->ixan", a_split, fetched, preferred_element_type=jnp.float32
    ).astype(jnp.bfloat16)
    slot_range = jnp.arange(slot_count, dtype=jnp.int32)
    summed = jnp.zeros((5 * aggregates, coarse_width, row_width), jnp.float32)
    for index_q in range(count_p):
        onehot = (t_slot[:, index_q][..., None] == slot_range).astype(jnp.bfloat16)
        total = jnp.zeros((elements, block, slot_count, coarse_width), jnp.float32)
        for index_p in range(count_p):
            lanes = product[:, :, :, index_p * coarse_width : (index_p + 1) * coarse_width]
            total = total + jnp.einsum(
                "ias,ixaz->ixsz",
                onehot[:, :, index_p, :],
                lanes,
                preferred_element_type=jnp.float32,
            )
        grouped = total.astype(jnp.bfloat16).reshape(elements, block, row_width)
        p_part = p_blocks[:, :, index_q * coarse_width : (index_q + 1) * coarse_width]
        term = jnp.einsum("ixw,ixn->iwn", p_part, grouped, preferred_element_type=jnp.float32)
        summed = summed + jax.ops.segment_sum(term, p_cols[:, index_q], num_segments=5 * aggregates)
    by_owner = summed.reshape(5, aggregates, coarse_width, row_width)
    result = by_owner[0]
    incoming = jnp.zeros((boundary, coarse_width, row_width), jnp.float32)
    for offset, which in ((-1, 1), (1, 2)):
        incoming = incoming + shifted(by_owner[which][:boundary], "gx", offset)
    for offset, which in ((-1, 3), (1, 4)):
        incoming = incoming + shifted(by_owner[which][:boundary], "yz", offset)
    result = jnp.concatenate([result[:boundary] + incoming, result[boundary:]], axis=0)
    return result


def solution(mesh):
    placed = (
        P(("gx", "yz"), None, None),
        P(("gx", "yz"), None, None),
        P(("gx", "yz"), None),
        P(("gx", "yz"), None, None),
        P(("gx", "yz"), None),
        P(("gx", "yz"), None, None, None),
    )
    return jax.shard_map(
        shards, mesh=mesh, in_specs=placed, out_specs=P(("gx", "yz"), None, None), check_vma=False
    )
```

profile of v0, /device:TPU:1, one launch (start us, length us, event | category | flops | bytes accessed | tf_op | source)
XLA Modules:
  0.0 170.7 jit_solution(12485837311793719010)
XLA Ops:
  0.0 2.6 %collective-permute-start = (bf16[16,64,192]{2,1,0:T(8,128)(2,1)}, bf16[16,64,192]{2,1,0:T(8,128)(2,1)}, u32[]{:S(2)}, u32[]{:S(2)}) collective-permute-start(bf16[16,64,192]{2,1,0:T(8,128)(2,1)} %param.9), channel_id=1, source_target_pairs={{0,16},{16,32},{32,48},{48,64},{64,80},{80,96},{96,112},{112,128},... | collective-permute-start | bytes 1179656 | tf_op jit(solution)/shard_map/ppermute | solution.py:12
  2.6 0.6 collective-permute-start.1
  3.2 1.8 %collective-permute-start.2 = (bf16[16,64,192]{2,1,0:T(8,128)(2,1)}, bf16[16,64,192]{2,1,0:T(8,128)(2,1)}, u32[]{:S(2)}, u32[]{:S(2)}) collective-permute-start(bf16[16,64,192]{2,1,0:T(8,128)(2,1)} %param.9), channel_id=1, source_target_pairs={{0,1},{1,2},{2,3},{3,4},{4,5},{5,6},{6,7},{7,8},{8,9},{9,10},{10,1... | collective-permute-start | bytes 1179656 | tf_op jit(solution)/shard_map/ppermute | solution.py:12
  5.0 5.3 %collective-permute-start.3 = (bf16[16,64,192]{2,1,0:T(8,128)(2,1)}, bf16[16,64,192]{2,1,0:T(8,128)(2,1)}, u32[]{:S(2)}, u32[]{:S(2)}) collective-permute-start(bf16[16,64,192]{2,1,0:T(8,128)(2,1)} %param.9), channel_id=1, source_target_pairs={{0,15},{1,0},{2,1},{3,2},{4,3},{5,4},{6,5},{7,6},{8,7},{9,8},{10,9... | collective-permute-start | bytes 1179656 | tf_op jit(solution)/shard_map/ppermute | solution.py:12
  10.3 0.7 compare_select_fusion
  11.0 0.7 compare_and_fusion
  11.7 1.4 compare_and_fusion.1
  13.1 0.6 pad_clamp_fusion.3
  13.7 0.7 slice_bitcast_fusion.18
  14.5 0.1 copy.42
  14.6 0.1 iota_compare_fusion
  14.7 0.1 copy.35
  14.8 0.1 iota_compare_fusion.1
  14.9 1.3 slice_bitcast_fusion.21
  16.3 0.1 iota_compare_fusion.2
  16.5 0.6 pad_clamp_fusion.2
  17.2 0.6 pad_clamp_fusion.1
  17.8 0.6 pad_clamp_fusion
  18.4 3.1 %reshape.49 = bf16[16,64,7,64]{3,2,1,0:T(8,128)(2,1)S(1)} reshape(bf16[16,64,448]{2,1,0:T(8,128)(2,1)} %param.8) | data formatting | bytes 1835008 | tf_op jit(solution)/shard_map/reshape | solution.py:35
  21.5 0.7 copy.25
  22.1 1.1 constant_dynamic-update-slice_fusion
  23.2 1.6 gather_fusion.1
  24.8 3.8 %collective-permute-done.1 = bf16[16,64,192]{2,1,0:T(8,128)(2,1)} collective-permute-done((bf16[16,64,192]{2,1,0:T(8,128)(2,1)}, bf16[16,64,192]{2,1,0:T(8,128)(2,1)}, u32[]{:S(2)}, u32[]{:S(2)}) %collective-permute-start.1) | collective-permute-done | bytes 393248 | tf_op jit(solution)/shard_map/ppermute | solution.py:12
  28.7 1.7 %gather_fusion.2 = bf16[4,64,192]{2,1,0:T(8,128)(2,1)S(1)} fusion(bf16[16,64,192]{2,1,0:T(8,128)(2,1)} %collective-permute-done.1, s32[1024]{0:T(1024)} %pad_clamp_fusion.3), kind=kCustom, calls=%fused_computation.1.clone | custom fusion | bytes 196624 | tf_op jit(solution)/shard_map/jit(_take)/gather | solution.py:29
  30.4 0.7 select_dynamic-update-slice_fusion.3
  31.1 1.4 collective-permute-done.2
  32.5 1.7 %gather_fusion.3 = bf16[4,64,192]{2,1,0:T(8,128)(2,1)S(1)} fusion(bf16[16,64,192]{2,1,0:T(8,128)(2,1)} %collective-permute-done.2, s32[1024]{0:T(1024)} %pad_clamp_fusion.2), kind=kCustom, calls=%fused_computation.2.clone | custom fusion | bytes 196624 | tf_op jit(solution)/shard_map/jit(_take)/gather | solution.py:32
  34.2 0.7 select_dynamic-update-slice_fusion.2
  34.9 0.7 select_dynamic-update-slice_fusion.1
  35.6 1.4 collective-permute-done.3
  37.1 1.7 %gather_fusion.4 = bf16[4,64,192]{2,1,0:T(8,128)(2,1)S(1)} fusion(bf16[16,64,192]{2,1,0:T(8,128)(2,1)} %collective-permute-done.3, s32[1024]{0:T(1024)} %pad_clamp_fusion.1), kind=kCustom, calls=%fused_computation.3.clone | custom fusion | bytes 196624 | tf_op jit(solution)/shard_map/jit(_take)/gather | solution.py:32
  38.8 0.7 select_dynamic-update-slice_fusion
  39.5 2.8 %gather_fusion = bf16[112,64,192]{2,1,0:T(8,128)(2,1)} fusion(bf16[32,64,192]{2,1,0:T(8,128)(2,1)S(1)} %select_dynamic-update-slice_fusion, s32[1024]{0:T(1024)} %pad_clamp_fusion), kind=kCustom, calls=%fused_computation.4 | custom fusion | bytes 5505472 | tf_op jit(solution)/shard_map/jit(_take)/gather | solution.py:34
  42.3 3.2 %convert_bitcast_fusion = bf16[16,64,7,192]{3,1,2,0:T(8,128)(2,1)S(1)} fusion(bf16[16,7,64,192]{3,2,1,0:T(8,128)(2,1)} %bitcast.99, pred[16,7]{1,0:T(8,128)(4,1)S(1)} %copy-done.1, bf16[16,64,7,64]{3,2,1,0:T(8,128)(2,1)S(1)} %reshape.49), kind=kOutput, calls=%fused_computation.14 | convolution fusion | flops 178913280 | bytes 6422640 | tf_op jit(solution)/shard_map/ixay,iayn->ixan/dot_general | solution.py:36
  45.5 1.3 fusion.29
  46.8 1.4 fusion.11
  48.2 4.6 %fusion.17 = f32[16,64,64,9]{2,3,1,0:T(8,128)} fusion(bf16[16,64,7,64]{3,1,2,0:T(8,128)(2,1)S(1)} %get-tuple-element.16, pred[16,7,3,9]{3,1,0,2:T(8,128)(4,1)S(1)} %iota_compare_fusion), kind=kOutput, calls=%fused_computation.27 | convolution fusion | flops 8257536 | bytes 4210688 | tf_op jit(solution)/shard_map/ias,ixaz->ixsz/dot_general | solution.py:46
  52.8 4.7 %fusion.13 = f32[16,64,64,9]{2,3,1,0:T(8,128)} fusion(bf16[16,64,7,64]{3,1,2,0:T(8,128)(2,1)S(1)} %get-tuple-element.15, pred[16,7,3,9]{3,1,0,2:T(8,128)(4,1)S(1)} %iota_compare_fusion.1), kind=kOutput, calls=%fused_computation.23 | convolution fusion | flops 8257536 | bytes 4210688 | tf_op jit(solution)/shard_map/ias,ixaz->ixsz/dot_general | solution.py:46
  57.5 4.7 %fusion.19 = f32[16,64,64,9]{2,3,1,0:T(8,128)} fusion(bf16[16,64,7,64]{3,1,2,0:T(8,128)(2,1)S(1)} %get-tuple-element.16, pred[16,7,3,9]{3,1,0,2:T(8,128)(4,1)S(1)} %iota_compare_fusion.1), kind=kOutput, calls=%fused_computation.29 | convolution fusion | flops 8257536 | bytes 4210688 | tf_op jit(solution)/shard_map/ias,ixaz->ixsz/dot_general | solution.py:46
  62.2 4.7 %fusion.15 = f32[16,64,64,9]{2,3,1,0:T(8,128)} fusion(bf16[16,64,7,64]{3,1,2,0:T(8,128)(2,1)S(1)} %get-tuple-element.15, pred[16,7,3,9]{3,1,0,2:T(8,128)(4,1)S(1)} %iota_compare_fusion.2), kind=kOutput, calls=%fused_computation.25 | convolution fusion | flops 8257536 | bytes 4210688 | tf_op jit(solution)/shard_map/ias,ixaz->ixsz/dot_general | solution.py:46
  66.8 4.7 %fusion.21 = f32[16,64,64,9]{2,3,1,0:T(8,128)} fusion(bf16[16,64,7,64]{3,1,2,0:T(8,128)(2,1)S(1)} %get-tuple-element.16, pred[16,7,3,9]{3,1,0,2:T(8,128)(4,1)S(1)} %iota_compare_fusion.2), kind=kOutput, calls=%fused_computation.31 | convolution fusion | flops 8257536 | bytes 4210688 | tf_op jit(solution)/shard_map/ias,ixaz->ixsz/dot_general | solution.py:46
  71.5 8.1 %fusion.2 = bf16[16,64,9,64]{3,2,1,0:T(8,128)(2,1)} fusion(f32[16,64,64,9]{2,3,1,0:T(8,128)} %fusion.17, f32[16,64,64,9]{2,3,1,0:T(8,128)S(1)} %fusion.11, bf16[16,64,7,64]{3,1,2,0:T(8,128)(2,1)S(1)} %get-tuple-element.14, pred[16,7,3,9]{3,1,0,2:T(8,128)(4,1)S(1)} %iota_compare_fusion), kind=kOutput, calls=%fused_computation.13 | convolution fusion | flops 10027008 | bytes 13778944 | tf_op jit(solution)/shard_map/ias,ixaz->ixsz/dot_general | solution.py:46
  79.6 6.2 %copy.46 = bf16[16,64,9,64]{1,3,2,0:T(8,128)(2,1)} copy(bf16[16,64,9,64]{3,2,1,0:T(8,128)(2,1)} %fusion.2) | data formatting | bytes 2359296 | tf_op jit(solution)/shard_map/convert_element_type | solution.py:52
  85.8 4.1 %convolution_bitcast_fusion = f32[16,64,576]{2,1,0:T(8,128)} fusion(bf16[16,64,576]{1,2,0:T(8,128)(2,1)} %bitcast.100, bf16[16,64,192]{2,1,0:T(8,128)(2,1)S(1)} %copy-done), kind=kOutput, calls=%fused_computation.35 | convolution fusion | flops 75497472 | bytes 3801088 | tf_op jit(solution)/shard_map/ixw,ixn->iwn/dot_general | solution.py:54
  89.9 10.1 %fusion.1 = bf16[16,64,9,64]{3,2,1,0:T(8,128)(2,1)} fusion(f32[16,64,64,9]{2,3,1,0:T(8,128)} %fusion.19, f32[16,64,64,9]{2,3,1,0:T(8,128)} %fusion.13, bf16[16,64,7,64]{3,1,2,0:T(8,128)(2,1)S(1)} %get-tuple-element.14, pred[16,7,3,9]{3,1,0,2:T(8,128)(4,1)S(1)} %iota_compare_fusion.1), kind=kOutput, calls=%fused_computation.12 | convolution fusion | flops 10027008 | bytes 7749632 | tf_op jit(solution)/shard_map/ias,ixaz->ixsz/dot_general | solution.py:46
  99.9 6.1 %copy.39 = bf16[16,64,9,64]{1,3,2,0:T(8,128)(2,1)} copy(bf16[16,64,9,64]{3,2,1,0:T(8,128)(2,1)} %fusion.1) | data formatting | bytes 2359296 | tf_op jit(solution)/shard_map/convert_element_type | solution.py:52
  106.0 4.3 %convolution_bitcast_fusion.1 = f32[16,64,576]{2,1,0:T(8,128)} fusion(bf16[16,64,576]{1,2,0:T(8,128)(2,1)} %bitcast.101, bf16[16,64,192]{2,1,0:T(8,128)(2,1)S(1)} %copy-done), kind=kOutput, calls=%fused_computation.36 | convolution fusion | flops 75497472 | bytes 3801088 | tf_op jit(solution)/shard_map/ixw,ixn->iwn/dot_general | solution.py:54
  110.3 9.9 %fusion = bf16[16,64,9,64]{3,2,1,0:T(8,128)(2,1)} fusion(f32[16,64,64,9]{2,3,1,0:T(8,128)} %fusion.21, f32[16,64,64,9]{2,3,1,0:T(8,128)} %fusion.15, bf16[16,64,7,64]{3,1,2,0:T(8,128)(2,1)S(1)} %get-tuple-element.14, pred[16,7,3,9]{3,1,0,2:T(8,128)(4,1)S(1)} %iota_compare_fusion.2), kind=kOutput, calls=%fused_computation.11 | convolution fusion | flops 10027008 | bytes 7749632 | tf_op jit(solution)/shard_map/ias,ixaz->ixsz/dot_general | solution.py:46
  120.2 5.7 %copy.32 = bf16[16,64,9,64]{1,3,2,0:T(8,128)(2,1)S(1)} copy(bf16[16,64,9,64]{3,2,1,0:T(8,128)(2,1)} %fusion) | data formatting | bytes 2359296 | tf_op jit(solution)/shard_map/convert_element_type | solution.py:52
  126.0 2.5 %convolution_bitcast_fusion.2 = f32[16,64,576]{2,1,0:T(8,128)} fusion(bf16[16,64,576]{1,2,0:T(8,128)(2,1)S(1)} %bitcast.102, bf16[16,64,192]{2,1,0:T(8,128)(2,1)S(1)} %copy-done), kind=kOutput, calls=%fused_computation.37 | convolution fusion | flops 75497472 | bytes 4980736 | tf_op jit(solution)/shard_map/ixw,ixn->iwn/dot_general | solution.py:54
  128.5 0.1 broadcast.19.clone.1
  128.6 3.9 %scatter_fusion.1 = f32[10,64,576]{2,1,0:T(8,128)S(1)} fusion(f32[10,64,576]{2,1,0:T(8,128)S(1)} %broadcast.19.clone.1, s32[16]{0:T(128)S(1)} %copy-done.4, f32[16,64,576]{2,1,0:T(8,128)} %convolution_bitcast_fusion.1), kind=kCustom, calls=%fused_computation.6 | custom fusion | flops 589824 | bytes 7077952 | tf_op jit(solution)/shard_map/scatter-add | solution.py:55
  132.6 0.1 broadcast.19.clone
  132.7 4.2 %scatter_fusion = f32[10,64,576]{2,1,0:T(8,128)S(1)} fusion(f32[10,64,576]{2,1,0:T(8,128)S(1)} %broadcast.19.clone, s32[16]{0:T(128)S(1)} %copy-done.3, f32[16,64,576]{2,1,0:T(8,128)} %convolution_bitcast_fusion.2), kind=kCustom, calls=%fused_computation.5 | custom fusion | flops 589824 | bytes 7077952 | tf_op jit(solution)/shard_map/scatter-add | solution.py:55
  136.9 1.4 add.64
  138.3 5.5 %scatter_fusion.2 = f32[10,64,576]{2,1,0:T(8,128)} fusion(f32[10,64,576]{2,1,0:T(8,128)} %add.64, s32[16]{0:T(128)S(1)} %copy-done.2, f32[16,64,576]{2,1,0:T(8,128)} %convolution_bitcast_fusion), kind=kCustom, calls=%fused_computation.7 | custom fusion | flops 589824 | bytes 7077952 | tf_op jit(solution)/shard_map/scatter-add | solution.py:55
  143.8 1.2 fusion.30
  145.0 3.8 %collective-permute-start.4 = (f32[1,64,576]{2,1,0:T(8,128)S(1)}, f32[1,64,576]{2,1,0:T(8,128)S(1)}, u32[]{:S(2)}, u32[]{:S(2)}) collective-permute-start(f32[1,64,576]{2,1,0:T(8,128)S(1)} %get-tuple-element.22), channel_id=1, source_target_pairs={{0,240},{16,0},{32,16},{48,32},{64,48},{80,64},{96,80},{112,96},{1... | collective-permute-start | bytes 442376 | tf_op jit(solution)/shard_map/ppermute | solution.py:12
  148.8 1.3 collective-permute-start.5
  150.1 9.6 %collective-permute-start.6 = (f32[1,64,576]{2,1,0:T(8,128)S(1)}, f32[1,64,576]{2,1,0:T(8,128)S(1)}, u32[]{:S(2)}, u32[]{:S(2)}) collective-permute-start(f32[1,64,576]{2,1,0:T(8,128)S(1)} %get-tuple-element.21), channel_id=1, source_target_pairs={{0,15},{1,0},{2,1},{3,2},{4,3},{5,4},{6,5},{7,6},{8,7},{9,8},{10,9... | collective-permute-start | bytes 442376 | tf_op jit(solution)/shard_map/ppermute | solution.py:12
  159.7 3.4 %collective-permute-done.6 = f32[1,64,576]{2,1,0:T(8,128)S(1)} collective-permute-done((f32[1,64,576]{2,1,0:T(8,128)S(1)}, f32[1,64,576]{2,1,0:T(8,128)S(1)}, u32[]{:S(2)}, u32[]{:S(2)}) %collective-permute-start.6) | collective-permute-done | bytes 147488 | tf_op jit(solution)/shard_map/ppermute | solution.py:12
  163.2 5.8 %collective-permute-done.7 = f32[1,64,576]{2,1,0:T(8,128)S(1)} collective-permute-done((f32[1,64,576]{2,1,0:T(8,128)S(1)}, f32[1,64,576]{2,1,0:T(8,128)S(1)}, u32[]{:S(2)}, u32[]{:S(2)}) %collective-permute-start.7) | collective-permute-done | bytes 147488 | tf_op jit(solution)/shard_map/ppermute | solution.py:12
  168.9 1.1 slice_add_fusion
  170.0 0.7 pad_maximum_fusion
  (18 shorter events, 0.3 us)
Async XLA Ops:
  0.0 23.2 %collective-permute-start = (bf16[16,64,192]{2,1,0:T(8,128)(2,1)}, bf16[16,64,192]{2,1,0:T(8,128)(2,1)}, u32[]{:S(2)}, u32[]{:S(2)}) collective-permute-start(bf16[16,64,192]{2,1,0:T(8,128)(2,1)} %param.9), channel_id=1, source_target_pairs={{0,16},{16,32},{32,48},{48,64},{64,80},{80,96},{96,112},{112,128},... | collective-permute-start | bytes 1179656 | tf_op jit(solution)/shard_map/ppermute | solution.py:12
  2.6 26.1 %collective-permute-start.1 = (bf16[16,64,192]{2,1,0:T(8,128)(2,1)}, bf16[16,64,192]{2,1,0:T(8,128)(2,1)}, u32[]{:S(2)}, u32[]{:S(2)}) collective-permute-start(bf16[16,64,192]{2,1,0:T(8,128)(2,1)} %param.9), channel_id=1, source_target_pairs={{0,240},{16,0},{32,16},{48,32},{64,48},{80,64},{96,80},{112,96},{1... | collective-permute-start | bytes 1179656 | tf_op jit(solution)/shard_map/ppermute | solution.py:12
  3.2 29.3 %collective-permute-start.2 = (bf16[16,64,192]{2,1,0:T(8,128)(2,1)}, bf16[16,64,192]{2,1,0:T(8,128)(2,1)}, u32[]{:S(2)}, u32[]{:S(2)}) collective-permute-start(bf16[16,64,192]{2,1,0:T(8,128)(2,1)} %param.9), channel_id=1, source_target_pairs={{0,1},{1,2},{2,3},{3,4},{4,5},{5,6},{6,7},{7,8},{8,9},{9,10},{10,1... | collective-permute-start | bytes 1179656 | tf_op jit(solution)/shard_map/ppermute | solution.py:12
  5.0 32.0 %collective-permute-start.3 = (bf16[16,64,192]{2,1,0:T(8,128)(2,1)}, bf16[16,64,192]{2,1,0:T(8,128)(2,1)}, u32[]{:S(2)}, u32[]{:S(2)}) collective-permute-start(bf16[16,64,192]{2,1,0:T(8,128)(2,1)} %param.9), channel_id=1, source_target_pairs={{0,15},{1,0},{2,1},{3,2},{4,3},{5,4},{6,5},{7,6},{8,7},{9,8},{10,9... | collective-permute-start | bytes 1179656 | tf_op jit(solution)/shard_map/ppermute | solution.py:12
  39.5 2.8 %copy-start.1 = (pred[16,7]{1,0:T(8,128)(4,1)S(1)}, pred[16,7]{1,0:T(8,128)(4,1)}, u32[]{:S(2)}) copy-start(pred[16,7]{1,0:T(8,128)(4,1)} %copy.25) | copy-start | bytes 340
  79.6 6.2 %copy-start = (bf16[16,64,192]{2,1,0:T(8,128)(2,1)S(1)}, bf16[16,64,192]{2,1,0:T(8,128)(2,1)}, u32[]{:S(2)}) copy-start(bf16[16,64,192]{2,1,0:T(8,128)(2,1)} %param.9) | copy-start | bytes 1179652
  126.0 2.7 %copy-start.4 = (s32[16]{0:T(128)S(1)}, s32[16]{0:T(128)}, u32[]{:S(2)}) copy-start(s32[16]{0:T(128)} %get-tuple-element.28) | copy-start | bytes 196
  128.6 4.1 %copy-start.3 = (s32[16]{0:T(128)S(1)}, s32[16]{0:T(128)}, u32[]{:S(2)}) copy-start(s32[16]{0:T(128)} %get-tuple-element.27) | copy-start | bytes 196
  136.9 1.4 copy-start.2
  145.0 14.7 %collective-permute-start.4 = (f32[1,64,576]{2,1,0:T(8,128)S(1)}, f32[1,64,576]{2,1,0:T(8,128)S(1)}, u32[]{:S(2)}, u32[]{:S(2)}) collective-permute-start(f32[1,64,576]{2,1,0:T(8,128)S(1)} %get-tuple-element.22), channel_id=1, source_target_pairs={{0,240},{16,0},{32,16},{48,32},{64,48},{80,64},{96,80},{112,96},{1... | collective-permute-start | bytes 442376 | tf_op jit(solution)/shard_map/ppermute | solution.py:12
  148.8 10.9 %collective-permute-start.5 = (f32[1,64,576]{2,1,0:T(8,128)S(1)}, f32[1,64,576]{2,1,0:T(8,128)S(1)}, u32[]{:S(2)}, u32[]{:S(2)}) collective-permute-start(f32[1,64,576]{2,1,0:T(8,128)S(1)} %get-tuple-element.19), channel_id=1, source_target_pairs={{0,16},{16,32},{32,48},{48,64},{64,80},{80,96},{96,112},{112,128},... | collective-permute-start | bytes 442376 | tf_op jit(solution)/shard_map/ppermute | solution.py:12
  150.1 13.0 %collective-permute-start.6 = (f32[1,64,576]{2,1,0:T(8,128)S(1)}, f32[1,64,576]{2,1,0:T(8,128)S(1)}, u32[]{:S(2)}, u32[]{:S(2)}) collective-permute-start(f32[1,64,576]{2,1,0:T(8,128)S(1)} %get-tuple-element.21), channel_id=1, source_target_pairs={{0,15},{1,0},{2,1},{3,2},{4,3},{5,4},{6,5},{7,6},{8,7},{9,8},{10,9... | collective-permute-start | bytes 442376 | tf_op jit(solution)/shard_map/ppermute | solution.py:12
  159.7 9.2 %collective-permute-start.7 = (f32[1,64,576]{2,1,0:T(8,128)S(1)}, f32[1,64,576]{2,1,0:T(8,128)S(1)}, u32[]{:S(2)}, u32[]{:S(2)}) collective-permute-start(f32[1,64,576]{2,1,0:T(8,128)S(1)} %get-tuple-element.20), channel_id=1, source_target_pairs={{0,1},{1,2},{2,3},{3,4},{4,5},{5,6},{6,7},{7,8},{8,9},{9,10},{10,1... | collective-permute-start | bytes 442376 | tf_op jit(solution)/shard_map/ppermute | solution.py:12
where the time goes:
time: 172 us; the launch traced here: 171 us
  matrix products  66.9 us (39%)
  local copies, waits for them, and re-layouts  37.6 us (22%)
  other arithmetic  25.1 us (15%)
  starting transfers between devices  25 us (15%)
  waiting for transfers between devices  15.8 us (9%)
    dot_general x9, matrix products, shards(): jnp.einsum('ias,ixaz->ixsz', onehot[:, :, index_p, :], lanes, preferred_e...  52.8 us
    ppermute x8, starting transfers between devices, shifted(): return lax.ppermute(value, axis, pairs)  25 us
    convert_element_type x3, local copies, waits for them, and re-layouts, shards(): grouped = total.astype(jnp.bfloat16).reshape(elements, block, row_width)  18 us
    ppermute x8, waiting for transfers between devices, shifted(): return lax.ppermute(value, axis, pairs)  15.8 us
    scatter-add x3, other arithmetic, shards(): jax.ops.segment_sum(term, p_cols[:, index_q], num_segments=5 * aggregates)  13.6 us
    dot_general x3, matrix products, shards(): jnp.einsum('ixw,ixn->iwn', p_part, grouped, preferred_element_type=jnp.fl...  10.9 us
  transfers between devices with their start and end apart: 8, of which 5 were waited for; matrix products, arithmetic and copies ran while one was open for 12% of the time, Pallas kernels for 0%

commit v1 on v0

v1 whole, which is shorter than its diff:
```python
import jax
import jax.numpy as jnp
from jax import lax
from jax.experimental import pallas as pl
from jax.experimental.pallas import tpu as pltpu
from jax.sharding import PartitionSpec as P

KC = 9
HALF = 32
OWN = 2
F32 = jnp.float32
BF16 = jnp.bfloat16
VMEM = pl.BlockSpec(memory_space=pltpu.VMEM)
SMEM = pl.BlockSpec(memory_space=pltpu.SMEM)


def params(mib=16):
    return pltpu.CompilerParams(vmem_limit_bytes=mib << 20)


def cost(flops, moved):
    return pl.CostEstimate(flops=flops, bytes_accessed=moved, transcendentals=0)


def swapped(value, axis, odd):
    count = lax.axis_size(axis)
    pairs = []
    for low in range(odd, count + odd, 2):
        first, second = low % count, (low + 1) % count
        pairs += [(first, second), (second, first)]
    return lax.ppermute(value, axis, pairs)


def gather_rows(sides, cross, near, far, p_blocks, to_cross, to_near, to_far):
    side_g, side_y = sides[0], sides[1]
    for asked, row, out in ((cross, 1 - side_g, to_cross), (near, 2 + side_y, to_near), (far, 3 - side_y, to_far)):
        for h in range(4):
            out[h] = p_blocks[asked[0, row, h]]


def doubled(block):
    return jnp.concatenate([block, block], axis=1)


def spread(rows, out, index):
    lane = lax.broadcasted_iota(jnp.int32, (64, 128), 1)
    low = lane < 64
    for p in range(3):
        wide = doubled(rows[:, p * 64 : (p + 1) * 64])
        zero = jnp.zeros_like(wide)
        out[index, 0:64, p * 128 : (p + 1) * 128] = jnp.where(low, wide, zero)
        out[index, 64:128, p * 128 : (p + 1) * 128] = jnp.where(low, zero, wide)


def restrict(a_blocks, p_blocks, left, local):
    def body(i, carry):
        rows = p_blocks[i]
        spread(rows, local, i)
        full = lax.dot_general(rows, a_blocks[i], (((0,), (0,)), ((), ())), preferred_element_type=F32).astype(BF16)
        top = jnp.concatenate([full[q * 64 : q * 64 + 32] for q in range(3)], axis=0)
        bottom = jnp.concatenate([full[q * 64 + 32 : q * 64 + 64] for q in range(3)], axis=0)
        for a in range(7):
            left[i, :, a * 128 : (a + 1) * 128] = jnp.concatenate(
                [top[:, a * 64 : (a + 1) * 64], bottom[:, a * 64 : (a + 1) * 64]], axis=1
            )
        return carry

    lax.fori_loop(0, 16, body, 0)


def outward(table, sides, wanted, left, local, chip, cross, near, far, o0, o1, o2, o3, halo, acc0, acc1, acc2):
    accs = (acc0, acc1, acc2)
    for acc in accs:
        acc[...] = jnp.zeros_like(acc)
    row = 1 - sides[0]
    for h in range(4):
        spread(chip[wanted[0, row, h]], halo, h)
        spread(cross[h], halo, 4 + h)
        spread(near[h], halo, 8 + h)
        spread(far[h], halo, 12 + h)

    def body(i, carry):
        for q in range(3):

            @pl.when(table[i, 70 + q] >= OWN)
            def _():
                for a in range(7):
                    slot = table[i, 63 + a]
                    piece = left[i, q * HALF : (q + 1) * HALF, a * 128 : (a + 1) * 128]
                    right = jnp.where(slot < 16, local[jnp.minimum(slot, 15)], halo[jnp.maximum(slot - 16, 0)])
                    value = jnp.dot(piece, right, preferred_element_type=F32)
                    for p in range(3):
                        where = table[i, (q * 7 + a) * 3 + p] - OWN * KC
                        accs[p][where] = accs[p][where] + value[:, p * 128 : (p + 1) * 128]

        return carry

    lax.fori_loop(0, 16, body, 0)
    for k, out in enumerate((o0, o1, o2, o3)):
        part = slice(k * KC, (k + 1) * KC)
        out[...] = (acc0[part] + acc1[part] + acc2[part]).astype(BF16)


def inward(table, left, local, halo, out, acc0, acc1, acc2):
    accs = (acc0, acc1, acc2)
    for acc in accs:
        acc[...] = jnp.zeros_like(acc)

    def body(i, carry):
        for a in range(7):
            slot = table[i, 63 + a]
            right = jnp.where(slot < 16, local[jnp.minimum(slot, 15)], halo[jnp.maximum(slot - 16, 0)])
            value = jnp.dot(left[i, :, a * 128 : (a + 1) * 128], right, preferred_element_type=F32)
            for q in range(3):
                for p in range(3):
                    where = jnp.minimum(table[i, (q * 7 + a) * 3 + p], OWN * KC)
                    accs[p][where] = accs[p][where] + value[q * HALF : (q + 1) * HALF, p * 128 : (p + 1) * 128]
        return carry

    lax.fori_loop(0, 16, body, 0)
    part = slice(0, OWN * KC)
    out[...] = acc0[part] + acc1[part] + acc2[part]


def finish(own, r0, r1, r2, r3, out):
    for c in range(OWN):
        for s in range(KC):
            value = own[c * KC + s]
            if c == 0:
                for r in (r0, r1, r2, r3):
                    value = value + r[s].astype(F32)
            out[c, 0:HALF, s * 64 : (s + 1) * 64] = value[:, 0:64]
            out[c, HALF:64, s * 64 : (s + 1) * 64] = value[:, 64:128]


def shards(a_blocks, p_blocks, a_slot, halo_rows, p_cols, t_slot):
    side_g = lax.axis_index("gx") % 2
    side_y = lax.axis_index("yz") % 2
    sides = jnp.stack([side_g, side_y]).astype(jnp.int32)
    cross_ask = swapped(halo_rows, "gx", 1)
    near_ask = swapped(halo_rows, "yz", 0)
    far_ask = swapped(halo_rows, "yz", 1)
    chip = swapped(p_blocks, "gx", 0)

    flip_g, flip_y = 4 * (1 - side_g), 4 * (1 - side_y)
    slots = jnp.where(a_slot < 16, a_slot, a_slot ^ jnp.where(a_slot < 24, flip_g, flip_y))
    heading = (p_cols // 2 - 1) * 4
    heading = (heading ^ jnp.where(heading < 8, flip_g, flip_y)) // 4
    target = jnp.where(p_cols < 2, p_cols, 2 + heading)
    bins = (target[:, :, None, None] * KC + t_slot).reshape(16, 63)
    table = jnp.concatenate([bins, slots, target], axis=1)

    piece = jax.ShapeDtypeStruct((4, 64, 192), BF16)
    to_cross, to_near, to_far = pl.pallas_call(
        gather_rows, out_shape=[piece] * 3, in_specs=[SMEM] * 4 + [VMEM], out_specs=[VMEM] * 3,
        compiler_params=params(2), cost_estimate=cost(0, 700000), name="gather_rows",
    )(sides, cross_ask, near_ask, far_ask, p_blocks)
    cross = swapped(to_cross, "gx", 1)
    near = swapped(to_near, "yz", 0)
    far = swapped(to_far, "yz", 1)

    left, local = pl.pallas_call(
        restrict,
        out_shape=[jax.ShapeDtypeStruct((16, 96, 896), BF16), jax.ShapeDtypeStruct((16, 128, 384), BF16)],
        in_specs=[VMEM] * 2, out_specs=[VMEM] * 2,
        compiler_params=params(), cost_estimate=cost(400000000, 6000000), name="restrict",
    )(a_blocks, p_blocks)

    packed = jax.ShapeDtypeStruct((KC, HALF, 128), BF16)
    outs = pl.pallas_call(
        outward,
        out_shape=[packed] * 4 + [jax.ShapeDtypeStruct((16, 128, 384), BF16)],
        in_specs=[SMEM] * 3 + [VMEM] * 6, out_specs=[VMEM] * 5,
        scratch_shapes=[pltpu.VMEM((4 * KC, HALF, 128), F32)] * 3,
        compiler_params=params(), cost_estimate=cost(400000000, 6000000), name="outward",
    )(table, sides, halo_rows, left, local, chip, cross, near, far)
    halo = outs[4]
    got = [swapped(outs[0], "gx", 0), swapped(outs[1], "gx", 1), swapped(outs[2], "yz", 0), swapped(outs[3], "yz", 1)]

    own = pl.pallas_call(
        inward,
        out_shape=jax.ShapeDtypeStruct((OWN * KC, HALF, 128), F32),
        in_specs=[SMEM] + [VMEM] * 3, out_specs=VMEM,
        scratch_shapes=[pltpu.VMEM((OWN * KC + 1, HALF, 128), F32)] * 3,
        compiler_params=params(), cost_estimate=cost(1000000000, 8000000), name="inward",
    )(table, left, local, halo)

    return pl.pallas_call(
        finish,
        out_shape=jax.ShapeDtypeStruct((OWN, 64, KC * 64), F32),
        in_specs=[VMEM] * 5, out_specs=VMEM,
        compiler_params=params(4), cost_estimate=cost(0, 1000000), name="finish",
    )(own, *got)


def solution(mesh):
    placed = (
        P(("gx", "yz"), None, None),
        P(("gx", "yz"), None, None),
        P(("gx", "yz"), None),
        P(("gx", "yz"), None, None),
        P(("gx", "yz"), None),
        P(("gx", "yz"), None, None, None),
    )
    return jax.shard_map(
        shards, mesh=mesh, in_specs=placed, out_specs=P(("gx", "yz"), None, None), check_vma=False
    )
```

time: 172 us -> 54.2 us (0.32)
  matrix products: 66.9 us -> 0 us
  local copies, waits for them, and re-layouts: 37.6 us -> 6.54 us
  other arithmetic: 25.1 us -> 0.95 us
  Pallas kernels: 0 us -> 16.2 us
  waiting for transfers between devices: 15.8 us -> 5.19 us
    dot_general x13 -> x0, matrix products: 66.9 us -> none  [the longest x9 52.8 us: shards(): jnp.einsum('ias,ixaz->ixsz', onehot[:, :, index_p, :], lanes, preferred_e...]
    convert_element_type x3 -> x0, local copies, waits for them, and re-layouts: 18 us -> none  [shards(): grouped = total.astype(jnp.bfloat16).reshape(elements, block, row_width)]
    pallas_call x0 -> x5, Pallas kernels: none -> 16.2 us  [the longest x1 5.78 us: shards(): pl.pallas_call(inward, out_shape=jax.ShapeDtypeStruct((OWN * KC, HALF, 12...]
    scatter-add x3 -> x0, other arithmetic: 13.6 us -> none  [shards(): jax.ops.segment_sum(term, p_cols[:, index_q], num_segments=5 * aggregates)]
    ppermute x8 -> x11, waiting for transfers between devices: 15.8 us -> 5.19 us  [swapped(): return lax.ppermute(value, axis, pairs)]
    gather x5 -> x0, local copies, waits for them, and re-layouts: 9.57 us -> none  [the longest x2 3.43 us: shards(): pieces.append(jnp.take(whole, wanted[2 if offset == 1 else 3], axis=0))]
    unnamed x11 -> x14, local copies, waits for them, and re-layouts: 1.1 us -> 6.36 us
    slice x3 -> x0, local copies, waits for them, and re-layouts: 3.79 us -> none  [the longest x1 1.34 us: shards(): p_cols[:, index_q]]
  transfers between devices with their start and end apart: 8 -> 11, of which waited for: 5 -> 3; matrix products, arithmetic and copies ran while one was open for 12% -> 5% of each run, Pallas kernels for 0% -> 21%
where the time goes in v1:
time: 54.2 us; the launch traced here: 53.5 us
  starting transfers between devices  24.4 us (45%)
  Pallas kernels  16.2 us (30%)
  local copies, waits for them, and re-layouts  6.54 us (12%)
  waiting for transfers between devices  5.19 us (10%)
  other arithmetic  0.95 us (2%)
    ppermute x11, starting transfers between devices, swapped(): return lax.ppermute(value, axis, pairs)  24.4 us
    unnamed x14, local copies, waits for them, and re-layouts  6.36 us
    pallas_call x1, Pallas kernels, shards(): pl.pallas_call(inward, out_shape=jax.ShapeDtypeStruct((OWN * KC, HALF, 12...  5.78 us
    ppermute x11, waiting for transfers between devices, swapped(): return lax.ppermute(value, axis, pairs)  5.19 us
    pallas_call x1, Pallas kernels, shards(): pl.pallas_call(restrict, out_shape=[jax.ShapeDtypeStruct((16, 96, 896), B...  4.98 us
    pallas_call x1, Pallas kernels, shards(): pl.pallas_call(outward, out_shape=[packed] * 4 + [jax.ShapeDtypeStruct((1...  3.94 us
  transfers between devices with their start and end apart: 11, of which 3 were waited for; matrix products, arithmetic and copies ran while one was open for 5% of the time, Pallas kernels for 21%

profile of v1, /device:TPU:1, one launch (start us, length us, event | category | flops | bytes accessed | tf_op | source)
XLA Modules:
  0.0 53.5 jit_solution(16951309938873820647)
XLA Ops:
  0.0 0.0 copy-start.5
  0.0 3.6 %collective-permute-start.2 = (s32[1,4,4]{2,1,0:T(4,128)}, s32[1,4,4]{2,1,0:T(4,128)S(1)}, u32[]{:S(2)}, u32[]{:S(2)}) collective-permute-start(s32[1,4,4]{2,1,0:T(4,128)} %wanted.1), channel_id=1, source_target_pairs={{0,1},{1,0},{2,3},{3,2},{4,5},{5,4},{6,7},{7,6},{8,9},{9,8},{10,11... | collective-permute-start | bytes 200 | tf_op jit(solution)/shard_map/ppermute | solution.py:31
  3.6 1.2 %collective-permute-start.1 = (s32[1,4,4]{2,1,0:T(4,128)}, s32[1,4,4]{2,1,0:T(4,128)S(1)}, u32[]{:S(2)}, u32[]{:S(2)}) collective-permute-start(s32[1,4,4]{2,1,0:T(4,128)} %wanted.1), channel_id=1, source_target_pairs={{16,32},{32,16},{48,64},{64,48},{80,96},{96,80},{112,128},{128,112... | collective-permute-start | bytes 200 | tf_op jit(solution)/shard_map/ppermute | solution.py:31
  4.7 7.0 %collective-permute-start.3 = (s32[1,4,4]{2,1,0:T(4,128)}, s32[1,4,4]{2,1,0:T(4,128)S(1)}, u32[]{:S(2)}, u32[]{:S(2)}) collective-permute-start(s32[1,4,4]{2,1,0:T(4,128)} %wanted.1), channel_id=1, source_target_pairs={{1,2},{2,1},{3,4},{4,3},{5,6},{6,5},{7,8},{8,7},{9,10},{10,9},{11,... | collective-permute-start | bytes 200 | tf_op jit(solution)/shard_map/ppermute | solution.py:31
  11.7 2.3 %collective-permute-start = (bf16[16,64,192]{2,1,0:T(8,128)(2,1)}, bf16[16,64,192]{2,1,0:T(8,128)(2,1)}, u32[]{:S(2)}, u32[]{:S(2)}) collective-permute-start(bf16[16,64,192]{2,1,0:T(8,128)(2,1)} %p_blocks.3), channel_id=1, source_target_pairs={{0,16},{16,0},{32,48},{48,32},{64,80},{80,64},{96,112},{112,96},{1... | collective-permute-start | bytes 1179656 | tf_op jit(solution)/shard_map/ppermute | solution.py:31
  14.0 0.8 %copy.32 = s32[16,3]{1,0:T(8,128)S(1)} copy(s32[16,3]{0,1:T(4,128)} %param.10) | data formatting | bytes 384 | tf_op args[4]
  14.8 0.1 copy.39
  14.9 0.8 %broadcast_add_fusion = s32[16,3,7,3]{0,2,3,1:T(8,128)S(1)} fusion(s32[16,3,7,3]{0,2,3,1:T(8,128)} %param.11, s32[16,3]{0,1:T(4,128)S(1)} %copy.39), kind=kLoop, calls=%fused_computation.2 | loop fusion | flops 1008 | bytes 8256 | tf_op jit(solution)/shard_map/add | solution.py:150
  15.7 0.1 pad_add_fusion.1.sides
  15.7 0.8 %copy.41 = s32[16,7]{1,0:T(8,128)S(1)} copy(s32[16,7]{0,1:T(8,128)} %param.8) | data formatting | bytes 896 | tf_op args[2]
  16.5 0.0 copy-start.2
  16.6 1.0 %copy-done.2 = bf16[16,64,192]{2,1,0:T(8,128)(2,1)S(1)} copy-done((bf16[16,64,192]{2,1,0:T(8,128)(2,1)S(1)}, bf16[16,64,192]{2,1,0:T(8,128)(2,1)}, u32[]{:S(2)}) %copy-start.2) | copy-done | bytes 393240
  17.6 0.0 copy-start.4
  17.6 1.2 %copy-done.4 = bf16[16,64,448]{2,1,0:T(8,128)(2,1)S(1)} copy-done((bf16[16,64,448]{2,1,0:T(8,128)(2,1)S(1)}, bf16[16,64,448]{2,1,0:T(8,128)(2,1)}, u32[]{:S(2)}) %copy-start.4) | copy-done | bytes 917528
  18.8 0.0 copy-start.3
  18.8 5.0 %restrict.1 = (bf16[16,96,896]{2,1,0:T(8,128)(2,1)S(1)}, bf16[16,128,384]{2,1,0:T(8,128)(2,1)S(1)}) custom-call(bf16[16,64,448]{2,1,0:T(8,128)(2,1)S(1)} %copy-done.4, bf16[16,64,192]{2,1,0:T(8,128)(2,1)S(1)} %copy-done.2), custom_call_target="tpu_custom_call" | custom-call | flops 400000000 | bytes 6000000 | tf_op jit(solution)/shard_map/restrict/pallas_call | solution.py:162
  23.8 0.0 copy-start
  23.8 1.2 %copy-done = bf16[16,128,384]{2,1,0:T(8,128)(2,1)} copy-done((bf16[16,128,384]{2,1,0:T(8,128)(2,1)}, bf16[16,128,384]{2,1,0:T(8,128)(2,1)S(1)}, u32[]{:S(2)}) %copy-start) | copy-done | bytes 1572888
  25.0 0.1 copy.45
  25.1 0.0 collective-permute-done.2.near
  25.1 0.0 collective-permute-done.1.cross
  25.1 0.0 collective-permute-done.3.far
  25.1 0.0 copy-done.3
  25.1 0.7 %gather_rows.1 = (bf16[4,64,192]{2,1,0:T(8,128)(2,1)S(1)}, bf16[4,64,192]{2,1,0:T(8,128)(2,1)S(1)}, bf16[4,64,192]{2,1,0:T(8,128)(2,1)S(1)}) custom-call(s32[2]{0:T(128)S(1)} %pad_add_fusion.1.sides, s32[1,4,4]{2,1,0:T(4,128)S(1)} %collective-permute-done.1.cross, s32[1,4,4]{2,1,0:T(4,128)S(1)} %collective-permute-done.2.near, ...), custom_call_target="tpu_custom_call" | custom-call | bytes 700000 | tf_op jit(solution)/shard_map/gather_rows/pallas_call | solution.py:154
  25.8 0.1 collective-permute-start.4
  25.9 0.1 collective-permute-start.5
  26.0 3.4 %collective-permute-start.6 = (bf16[4,64,192]{2,1,0:T(8,128)(2,1)S(1)}, bf16[4,64,192]{2,1,0:T(8,128)(2,1)S(1)}, u32[]{:S(2)}, u32[]{:S(2)}) collective-permute-start(bf16[4,64,192]{2,1,0:T(8,128)(2,1)S(1)} %get-tuple-element.19), channel_id=1, source_target_pairs={{1,2},{2,1},{3,4},{4,3},{5,6},{6,5},{7,8},{8,7},{9,10},{10,9},{11,... | collective-permute-start | bytes 294920 | tf_op jit(solution)/shard_map/ppermute | solution.py:31
  29.4 0.1 pad_add_fusion.table
  29.4 3.9 %collective-permute-done.4.cross = bf16[4,64,192]{2,1,0:T(8,128)(2,1)S(1)} collective-permute-done((bf16[4,64,192]{2,1,0:T(8,128)(2,1)S(1)}, bf16[4,64,192]{2,1,0:T(8,128)(2,1)S(1)}, u32[]{:S(2)}, u32[]{:S(2)}) %collective-permute-start.4) | collective-permute-done | bytes 98336 | tf_op jit(solution)/shard_map/ppermute | solution.py:31
  33.3 1.0 %collective-permute-done.5.near = bf16[4,64,192]{2,1,0:T(8,128)(2,1)S(1)} collective-permute-done((bf16[4,64,192]{2,1,0:T(8,128)(2,1)S(1)}, bf16[4,64,192]{2,1,0:T(8,128)(2,1)S(1)}, u32[]{:S(2)}, u32[]{:S(2)}) %collective-permute-start.5) | collective-permute-done | bytes 98336 | tf_op jit(solution)/shard_map/ppermute | solution.py:31
  34.3 0.3 collective-permute-done.6.far
  34.6 0.0 collective-permute-done.chip
  34.6 0.0 copy-done.5
  34.6 0.0 copy-start.1
  34.6 1.4 %copy-done.1 = bf16[16,128,384]{2,1,0:T(8,128)(2,1)S(1)} copy-done((bf16[16,128,384]{2,1,0:T(8,128)(2,1)S(1)}, bf16[16,128,384]{2,1,0:T(8,128)(2,1)}, u32[]{:S(2)}) %copy-start.1) | copy-done | bytes 1572888
  36.0 3.9 %outward.1 = (bf16[9,32,128]{2,1,0:T(8,128)(2,1)S(1)}, bf16[9,32,128]{2,1,0:T(8,128)(2,1)S(1)}, bf16[9,32,128]{2,1,0:T(8,128)(2,1)S(1)}, bf16[9,32,128]{2,1,0:T(8,128)(2,1)S(1)}, bf16[16,128,384]{2,1,0:T(8,128)(2,1)S(1)}) custom-call(s32[16,73]{1,0:T(8,128)S(1)} %pad_add_fusion.table, s32[2]{0:T(128)S(1)} %pad_add_fusion.1.sides, s32[1,4,4]{2,1,0:T(4,128)S(1)} %copy-done.5, ...), custom_call_target="tpu_custom_call" | custom-call | flops 400000000 | bytes 6000000 | tf_op jit(solution)/shard_map/outward/pallas_call | solution.py:170
  40.0 1.9 %collective-permute-start.7 = (bf16[9,32,128]{2,1,0:T(8,128)(2,1)S(1)}, bf16[9,32,128]{2,1,0:T(8,128)(2,1)S(1)}, u32[]{:S(2)}, u32[]{:S(2)}) collective-permute-start(bf16[9,32,128]{2,1,0:T(8,128)(2,1)S(1)} %get-tuple-element.21), channel_id=1, source_target_pairs={{0,16},{16,0},{32,48},{48,32},{64,80},{80,64},{96,112},{112,96},{1... | collective-permute-start | bytes 221192 | tf_op jit(solution)/shard_map/ppermute | solution.py:31
  41.9 0.6 %collective-permute-start.8 = (bf16[9,32,128]{2,1,0:T(8,128)(2,1)S(1)}, bf16[9,32,128]{2,1,0:T(8,128)(2,1)S(1)}, u32[]{:S(2)}, u32[]{:S(2)}) collective-permute-start(bf16[9,32,128]{2,1,0:T(8,128)(2,1)S(1)} %get-tuple-element.22), channel_id=1, source_target_pairs={{16,32},{32,16},{48,64},{64,48},{80,96},{96,80},{112,128},{128,112... | collective-permute-start | bytes 221192 | tf_op jit(solution)/shard_map/ppermute | solution.py:31
  42.4 3.3 %collective-permute-start.9 = (bf16[9,32,128]{2,1,0:T(8,128)(2,1)S(1)}, bf16[9,32,128]{2,1,0:T(8,128)(2,1)S(1)}, u32[]{:S(2)}, u32[]{:S(2)}) collective-permute-start(bf16[9,32,128]{2,1,0:T(8,128)(2,1)S(1)} %get-tuple-element.23), channel_id=1, source_target_pairs={{0,1},{1,0},{2,3},{3,2},{4,5},{5,4},{6,7},{7,6},{8,9},{9,8},{10,11... | collective-permute-start | bytes 221192 | tf_op jit(solution)/shard_map/ppermute | solution.py:31
  45.8 1.0 %collective-permute-start.10 = (bf16[9,32,128]{2,1,0:T(8,128)(2,1)S(1)}, bf16[9,32,128]{2,1,0:T(8,128)(2,1)S(1)}, u32[]{:S(2)}, u32[]{:S(2)}) collective-permute-start(bf16[9,32,128]{2,1,0:T(8,128)(2,1)S(1)} %get-tuple-element.24), channel_id=1, source_target_pairs={{1,2},{2,1},{3,4},{4,3},{5,6},{6,5},{7,8},{8,7},{9,10},{10,9},{11,... | collective-permute-start | bytes 221192 | tf_op jit(solution)/shard_map/ppermute | solution.py:31
  46.7 5.8 %inward.1.own = f32[18,32,128]{2,1,0:T(8,128)S(1)} custom-call(s32[16,73]{1,0:T(8,128)S(1)} %pad_add_fusion.table, bf16[16,96,896]{2,1,0:T(8,128)(2,1)S(1)} %get-tuple-element.15.left, bf16[16,128,384]{2,1,0:T(8,128)(2,1)S(1)} %copy-done.1, bf16[16,128,384]{2,1,0:T(8,128)(2,1)S(1)} %get-tuple-element.20.halo), custom_call_target="tpu_custom_call" | custom-call | flops 1000000000 | bytes 8000000 | tf_op jit(solution)/shard_map/inward/pallas_call | solution.py:180
  52.5 0.0 collective-permute-done.7.r0
  52.5 0.0 collective-permute-done.8.r1
  52.5 0.0 collective-permute-done.9.r2
  52.6 0.0 collective-permute-done.10.r3
  52.6 0.9 %finish.1 = f32[2,64,576]{2,1,0:T(8,128)} custom-call(f32[18,32,128]{2,1,0:T(8,128)S(1)} %inward.1.own, bf16[9,32,128]{2,1,0:T(8,128)(2,1)S(1)} %collective-permute-done.7.r0, bf16[9,32,128]{2,1,0:T(8,128)(2,1)S(1)} %collective-permute-done.8.r1, bf16[9,32,128]{2,1,0:T(8,128)(2,1)S(1)} %collective-permute-done.9.r2, ...), custom_call_target="tpu_custom_call" | custom-call | bytes 1000000 | tf_op jit(solution)/shard_map/finish/pallas_call | solution.py:188
  (4 shorter events, 0.1 us)
Async XLA Ops:
  0.0 34.6 %copy-start.5 = (s32[1,4,4]{2,1,0:T(4,128)S(1)}, s32[1,4,4]{2,1,0:T(4,128)}, u32[]{:S(2)}) copy-start(s32[1,4,4]{2,1,0:T(4,128)} %wanted.1) | copy-start | bytes 196
  0.0 25.1 %collective-permute-start.2 = (s32[1,4,4]{2,1,0:T(4,128)}, s32[1,4,4]{2,1,0:T(4,128)S(1)}, u32[]{:S(2)}, u32[]{:S(2)}) collective-permute-start(s32[1,4,4]{2,1,0:T(4,128)} %wanted.1), channel_id=1, source_target_pairs={{0,1},{1,0},{2,3},{3,2},{4,5},{5,4},{6,7},{7,6},{8,9},{9,8},{10,11... | collective-permute-start | bytes 200 | tf_op jit(solution)/shard_map/ppermute | solution.py:31
  3.6 21.5 %collective-permute-start.1 = (s32[1,4,4]{2,1,0:T(4,128)}, s32[1,4,4]{2,1,0:T(4,128)S(1)}, u32[]{:S(2)}, u32[]{:S(2)}) collective-permute-start(s32[1,4,4]{2,1,0:T(4,128)} %wanted.1), channel_id=1, source_target_pairs={{16,32},{32,16},{48,64},{64,48},{80,96},{96,80},{112,128},{128,112... | collective-permute-start | bytes 200 | tf_op jit(solution)/shard_map/ppermute | solution.py:31
  4.7 20.3 %collective-permute-start.3 = (s32[1,4,4]{2,1,0:T(4,128)}, s32[1,4,4]{2,1,0:T(4,128)S(1)}, u32[]{:S(2)}, u32[]{:S(2)}) collective-permute-start(s32[1,4,4]{2,1,0:T(4,128)} %wanted.1), channel_id=1, source_target_pairs={{1,2},{2,1},{3,4},{4,3},{5,6},{6,5},{7,8},{8,7},{9,10},{10,9},{11,... | collective-permute-start | bytes 200 | tf_op jit(solution)/shard_map/ppermute | solution.py:31
  11.7 22.9 %collective-permute-start = (bf16[16,64,192]{2,1,0:T(8,128)(2,1)}, bf16[16,64,192]{2,1,0:T(8,128)(2,1)}, u32[]{:S(2)}, u32[]{:S(2)}) collective-permute-start(bf16[16,64,192]{2,1,0:T(8,128)(2,1)} %p_blocks.3), channel_id=1, source_target_pairs={{0,16},{16,0},{32,48},{48,32},{64,80},{80,64},{96,112},{112,96},{1... | collective-permute-start | bytes 1179656 | tf_op jit(solution)/shard_map/ppermute | solution.py:31
  16.5 1.0 %copy-start.2 = (bf16[16,64,192]{2,1,0:T(8,128)(2,1)S(1)}, bf16[16,64,192]{2,1,0:T(8,128)(2,1)}, u32[]{:S(2)}) copy-start(bf16[16,64,192]{2,1,0:T(8,128)(2,1)} %p_blocks.3) | copy-start | bytes 1179652
  17.6 1.2 %copy-start.4 = (bf16[16,64,448]{2,1,0:T(8,128)(2,1)S(1)}, bf16[16,64,448]{2,1,0:T(8,128)(2,1)}, u32[]{:S(2)}) copy-start(bf16[16,64,448]{2,1,0:T(8,128)(2,1)} %a_blocks.1) | copy-start | bytes 2752516
  18.8 6.3 %copy-start.3 = (bf16[16,64,192]{2,1,0:T(8,128)(2,1)S(1)}, bf16[16,64,192]{2,1,0:T(8,128)(2,1)}, u32[]{:S(2)}) copy-start(bf16[16,64,192]{2,1,0:T(8,128)(2,1)} %p_blocks.3) | copy-start | bytes 1179652
  23.8 1.2 %copy-start = (bf16[16,128,384]{2,1,0:T(8,128)(2,1)}, bf16[16,128,384]{2,1,0:T(8,128)(2,1)S(1)}, u32[]{:S(2)}) copy-start(bf16[16,128,384]{2,1,0:T(8,128)(2,1)S(1)} %get-tuple-element.16.local) | copy-start | bytes 4718596
  25.8 7.5 %collective-permute-start.4 = (bf16[4,64,192]{2,1,0:T(8,128)(2,1)S(1)}, bf16[4,64,192]{2,1,0:T(8,128)(2,1)S(1)}, u32[]{:S(2)}, u32[]{:S(2)}) collective-permute-start(bf16[4,64,192]{2,1,0:T(8,128)(2,1)S(1)} %get-tuple-element.17), channel_id=1, source_target_pairs={{16,32},{32,16},{48,64},{64,48},{80,96},{96,80},{112,128},{128,112... | collective-permute-start | bytes 294920 | tf_op jit(solution)/shard_map/ppermute | solution.py:31
  25.9 8.4 %collective-permute-start.5 = (bf16[4,64,192]{2,1,0:T(8,128)(2,1)S(1)}, bf16[4,64,192]{2,1,0:T(8,128)(2,1)S(1)}, u32[]{:S(2)}, u32[]{:S(2)}) collective-permute-start(bf16[4,64,192]{2,1,0:T(8,128)(2,1)S(1)} %get-tuple-element.18), channel_id=1, source_target_pairs={{0,1},{1,0},{2,3},{3,2},{4,5},{5,4},{6,7},{7,6},{8,9},{9,8},{10,11... | collective-permute-start | bytes 294920 | tf_op jit(solution)/shard_map/ppermute | solution.py:31
  26.0 8.6 %collective-permute-start.6 = (bf16[4,64,192]{2,1,0:T(8,128)(2,1)S(1)}, bf16[4,64,192]{2,1,0:T(8,128)(2,1)S(1)}, u32[]{:S(2)}, u32[]{:S(2)}) collective-permute-start(bf16[4,64,192]{2,1,0:T(8,128)(2,1)S(1)} %get-tuple-element.19), channel_id=1, source_target_pairs={{1,2},{2,1},{3,4},{4,3},{5,6},{6,5},{7,8},{8,7},{9,10},{10,9},{11,... | collective-permute-start | bytes 294920 | tf_op jit(solution)/shard_map/ppermute | solution.py:31
  34.6 1.4 %copy-start.1 = (bf16[16,128,384]{2,1,0:T(8,128)(2,1)S(1)}, bf16[16,128,384]{2,1,0:T(8,128)(2,1)}, u32[]{:S(2)}) copy-start(bf16[16,128,384]{2,1,0:T(8,128)(2,1)} %copy-done) | copy-start | bytes 4718596
  40.0 12.6 %collective-permute-start.7 = (bf16[9,32,128]{2,1,0:T(8,128)(2,1)S(1)}, bf16[9,32,128]{2,1,0:T(8,128)(2,1)S(1)}, u32[]{:S(2)}, u32[]{:S(2)}) collective-permute-start(bf16[9,32,128]{2,1,0:T(8,128)(2,1)S(1)} %get-tuple-element.21), channel_id=1, source_target_pairs={{0,16},{16,0},{32,48},{48,32},{64,80},{80,64},{96,112},{112,96},{1... | collective-permute-start | bytes 221192 | tf_op jit(solution)/shard_map/ppermute | solution.py:31
  41.9 10.7 %collective-permute-start.8 = (bf16[9,32,128]{2,1,0:T(8,128)(2,1)S(1)}, bf16[9,32,128]{2,1,0:T(8,128)(2,1)S(1)}, u32[]{:S(2)}, u32[]{:S(2)}) collective-permute-start(bf16[9,32,128]{2,1,0:T(8,128)(2,1)S(1)} %get-tuple-element.22), channel_id=1, source_target_pairs={{16,32},{32,16},{48,64},{64,48},{80,96},{96,80},{112,128},{128,112... | collective-permute-start | bytes 221192 | tf_op jit(solution)/shard_map/ppermute | solution.py:31
  42.4 10.1 %collective-permute-start.9 = (bf16[9,32,128]{2,1,0:T(8,128)(2,1)S(1)}, bf16[9,32,128]{2,1,0:T(8,128)(2,1)S(1)}, u32[]{:S(2)}, u32[]{:S(2)}) collective-permute-start(bf16[9,32,128]{2,1,0:T(8,128)(2,1)S(1)} %get-tuple-element.23), channel_id=1, source_target_pairs={{0,1},{1,0},{2,3},{3,2},{4,5},{5,4},{6,7},{7,6},{8,9},{9,8},{10,11... | collective-permute-start | bytes 221192 | tf_op jit(solution)/shard_map/ppermute | solution.py:31
  45.8 6.8 %collective-permute-start.10 = (bf16[9,32,128]{2,1,0:T(8,128)(2,1)S(1)}, bf16[9,32,128]{2,1,0:T(8,128)(2,1)S(1)}, u32[]{:S(2)}, u32[]{:S(2)}) collective-permute-start(bf16[9,32,128]{2,1,0:T(8,128)(2,1)S(1)} %get-tuple-element.24), channel_id=1, source_target_pairs={{1,2},{2,1},{3,4},{4,3},{5,6},{6,5},{7,8},{8,7},{9,10},{10,9},{11,... | collective-permute-start | bytes 221192 | tf_op jit(solution)/shard_map/ppermute | solution.py:31

commit v2 on v1

v2 whole, which is shorter than its diff:
```python
import jax
import jax.numpy as jnp
from jax import lax
from jax.experimental import pallas as pl
from jax.experimental.pallas import tpu as pltpu
from jax.sharding import PartitionSpec as P


KC = 9
HALF = 32
OWN = 2
BINS = 6 * KC
F32 = jnp.float32
BF16 = jnp.bfloat16
VMEM = pl.BlockSpec(memory_space=pltpu.VMEM)
SMEM = pl.BlockSpec(memory_space=pltpu.SMEM)
ANY = pl.BlockSpec(memory_space=pl.ANY)
HBM = pl.BlockSpec(memory_space=pltpu.HBM)
GROUP = 14
AHEAD = 2
LEFT = jax.ShapeDtypeStruct((128, 96, 128), BF16)
RIGHT = jax.ShapeDtypeStruct((32, 3, 128, 128), BF16)
SUMS = [jax.ShapeDtypeStruct((BINS, HALF, 128), F32)] * 3


def params(mib=16):
    return pltpu.CompilerParams(vmem_limit_bytes=mib << 20)


def cost(flops, moved):
    return pl.CostEstimate(flops=flops, bytes_accessed=moved, transcendentals=0)


def swapped(value, axis, odd):
    count = lax.axis_size(axis)
    pairs = []
    for low in range(odd, count + odd, 2):
        first, second = low % count, (low + 1) % count
        pairs += [(first, second), (second, first)]
    return lax.ppermute(value, axis, pairs)


def gather_rows(sides, cross, near, far, p_blocks, to_cross, to_near, to_far):
    side_g, side_y = sides[0], sides[1]
    for asked, row, out in ((far, 3 - side_y, to_far), (cross, 1 - side_g, to_cross), (near, 2 + side_y, to_near)):
        for h in range(4):
            rows = p_blocks[asked[0, row, h]]
            out[h, 0:64] = rows[:, 0:128]
            out[h, 64:96] = jnp.concatenate([rows[0:32, 128:192], rows[32:64, 128:192]], axis=1)


def fetch(*refs):
    count = (len(refs) - 1) // 2
    copies = [pltpu.make_async_copy(refs[n], refs[count + n], refs[-1].at[n]) for n in range(count)]
    for copy in copies:
        copy.start()
    for copy in copies:
        copy.wait()


def turned(pair):
    return jnp.concatenate([pair[:, 64:128], pair[:, 0:64]], axis=1)


def spread(pair, last, right, index):
    low = lax.broadcasted_iota(jnp.int32, (64, 128), 1) < 64
    zero = jnp.zeros_like(pair)
    other = turned(pair)
    for p, first, second in ((0, pair, other), (1, other, pair)):
        right[index, p, 0:64] = jnp.where(low, first, zero)
        right[index, p, 64:128] = jnp.where(low, zero, second)
    low, zero, other = low[0:32], zero[0:32], turned(last)
    right[index, 2, 0:32] = jnp.where(low, last, zero)
    right[index, 2, 32:64] = jnp.where(low, other, zero)
    right[index, 2, 64:96] = jnp.where(low, zero, other)
    right[index, 2, 96:128] = jnp.where(low, zero, last)


def spread_rows(rows, right, index):
    last = jnp.concatenate([rows[0:32, 128:192], rows[32:64, 128:192]], axis=1)
    spread(rows[:, 0:128], last, right, index)


def add_pairs(pairs, places, t_slot, left, right, sums):
    for pair in pairs:
        i, a = pair >> 3, pair & 7
        slot = places[a, i]
        wide = jnp.concatenate([right[slot, p] for p in range(3)], axis=1)
        value = jnp.dot(left[pair], wide, preferred_element_type=F32)
        for q in range(3):
            first = places[7 + q, i]
            for p in range(3):
                where = first + t_slot[q, p, a, i]
                sums[p][where] = sums[p][where] + value[q * HALF : (q + 1) * HALF, p * 128 : (p + 1) * 128]


def later_pairs(lists, b):
    sent_far, shift_sent, going, kept_far, shift_kept = (lists[4, n] for n in range(5))
    pairs = []
    for j in range(GROUP):
        k = b * GROUP + j
        m = k - going
        row = jnp.where(k < sent_far, 2, jnp.where(m < 0, 0, jnp.where(m < kept_far, 3, 1)))
        near = jnp.where(k < sent_far, k, k + shift_sent)
        column = jnp.where(m < 0, near, jnp.where(m < kept_far, m, m + shift_kept))
        pairs.append(lists[row, column])
    return pairs


def early(
    sides, wanted, a_slot, p_cols, a_blocks, p_blocks, chip, after, t_slot,
    left, right, sum0, sum1, sum2, lists, places, held, rows4, sems,
):
    sums = (sum0, sum1, sum2)
    row = 1 - sides[0]
    flip_g, flip_y = 4 * (1 - sides[0]), 4 * (1 - sides[1])
    loads = [pltpu.make_async_copy(a_blocks.at[pl.ds(4 * c, 4)], held.at[pl.ds(4 * c, 4)], sems.at[c]) for c in range(4)]
    pulls = [pltpu.make_async_copy(chip.at[wanted[0, row, h]], rows4.at[h], sems.at[4 + h]) for h in range(4)]
    for copy in loads + pulls:
        copy.start()

    def clear(j, carry):
        for total in sums:
            total[j] = jnp.zeros((HALF, 128), F32)
        return carry

    lax.fori_loop(0, BINS, clear, 0)
    counts = [jnp.int32(0)] * 4
    for c in range(4):
        loads[c].wait()
        for i in range(4 * c, 4 * c + 4):
            rows = p_blocks[i]
            spread_rows(rows, right, i)
            full = lax.dot_general(rows, held[i], (((0,), (0,)), ((), ())), preferred_element_type=F32).astype(BF16)
            top = jnp.concatenate([full[q * 64 : q * 64 + 32] for q in range(3)], axis=0)
            bottom = jnp.concatenate([full[q * 64 + 32 : q * 64 + 64] for q in range(3)], axis=0)
            for q in range(3):
                aim = p_cols[q, i]
                side = ((aim >> 1) - 1) << 2
                side = (side ^ jnp.where(side < 8, flip_g, flip_y)) >> 2
                places[7 + q, i] = KC * jnp.where(aim < OWN, aim, OWN + side)
            sent = jnp.maximum(jnp.maximum(places[7, i], places[8, i]), places[9, i]) >= OWN * KC
            for a in range(7):
                pair = i * 8 + a
                left[pair] = jnp.concatenate([top[:, a * 64 : (a + 1) * 64], bottom[:, a * 64 : (a + 1) * 64]], axis=1)
                slot = a_slot[a, i]
                own = slot < 16
                places[a, i] = jnp.where(own, slot, slot ^ jnp.where(slot < 24, flip_g, flip_y))
                for kind, here in enumerate((own & sent, own & ~sent, ~own & sent, ~own & ~sent)):
                    lists[kind, counts[kind]] = pair
                    counts[kind] = counts[kind] + jnp.where(here, 1, 0)
    groups = jnp.minimum((counts[0] + counts[1]) // GROUP, AHEAD)
    done = groups * GROUP
    lists[4, 0] = counts[2]
    lists[4, 1] = jnp.minimum(done, counts[0]) - counts[2]
    lists[4, 2] = counts[2] + counts[0] - jnp.minimum(done, counts[0])
    lists[4, 3] = counts[3]
    lists[4, 4] = jnp.maximum(done - counts[0], 0) - counts[3]
    lists[4, 5] = 112 // GROUP - groups
    first = counts[0]
    for h in range(4):
        pulls[h].wait()
    for h in range(4):
        spread_rows(rows4[h], right, 16 + h)

    def body(b, carry):
        pairs = []
        for j in range(GROUP):
            k = b * GROUP + j
            head = k < first
            pairs.append(lists[jnp.where(head, 0, 1), jnp.where(head, k, k - first)])
        add_pairs(pairs, places, t_slot, left, right, sums)
        return carry

    lax.fori_loop(0, groups, body, 0)


def outward(
    places, t_slot, lists, left, right_in, s0, s1, s2, cross, near, far, o0, o1, o2, o3, right, sum0, sum1, sum2
):
    for h in range(4):
        for rows, base in ((cross, 20), (near, 24), (far, 28)):
            spread(rows[h, 0:64], rows[h, 64:96], right, base + h)
    going = lists[4, 2]

    def body(b, carry):
        pairs = later_pairs(lists, b)
        add_pairs(pairs, places, t_slot, left, right, (sum0, sum1, sum2))
        return carry

    lax.fori_loop(0, (going + GROUP - 1) // GROUP, body, 0)
    for k, out in enumerate((o0, o1, o2, o3)):
        part = pl.ds((OWN + k) * KC, KC)
        out[...] = (sum0[part] + sum1[part] + sum2[part]).astype(BF16)


def inward(places, t_slot, lists, left, right, s0, s1, s2, out, sum0, sum1, sum2):
    going = lists[4, 2]

    def body(b, carry):
        pairs = later_pairs(lists, b)
        add_pairs(pairs, places, t_slot, left, right, (sum0, sum1, sum2))
        return carry

    lax.fori_loop((going + GROUP - 1) // GROUP, lists[4, 5], body, 0)
    part = pl.ds(0, OWN * KC)
    out[...] = sum0[part] + sum1[part] + sum2[part]


def finish(own, r0, r1, r2, r3, out):
    for c in range(OWN):
        for s in range(KC):
            value = own[c * KC + s]
            if c == 0:
                for r in (r0, r1, r2, r3):
                    value = value + r[s].astype(F32)
            out[c, 0:HALF, s * 64 : (s + 1) * 64] = value[:, 0:64]
            out[c, HALF:64, s * 64 : (s + 1) * 64] = value[:, 64:128]


def shards(a_blocks, p_blocks, a_slot, halo_rows, p_cols, t_slot):
    side_g = lax.axis_index("gx") % 2
    side_y = lax.axis_index("yz") % 2
    sides = jnp.stack([side_g, side_y]).astype(jnp.int32)
    far_ask = swapped(halo_rows, "yz", 1)
    cross_ask = swapped(halo_rows, "gx", 1)
    near_ask = swapped(halo_rows, "yz", 0)
    chip = swapped(p_blocks, "gx", 0)

    sources = [p_blocks, halo_rows, a_slot.T, p_cols.T, t_slot.transpose(1, 3, 2, 0)]
    held, wanted, a_slot, p_cols, t_slot = pl.pallas_call(
        fetch, out_shape=[jax.ShapeDtypeStruct(x.shape, x.dtype) for x in sources],
        in_specs=[HBM] * 5, out_specs=[VMEM] * 5, scratch_shapes=[pltpu.SemaphoreType.DMA((5,))],
        compiler_params=params(2), cost_estimate=cost(0, 800000), name="fetch",
    )(*[pltpu.with_memory_space_constraint(x, pltpu.HBM) for x in sources])
    piece = jax.ShapeDtypeStruct((4, 96, 128), BF16)
    to_cross, to_near, to_far = pl.pallas_call(
        gather_rows, out_shape=[piece] * 3, in_specs=[SMEM] * 4 + [VMEM], out_specs=[VMEM] * 3,
        compiler_params=params(2), cost_estimate=cost(0, 700000), name="gather_rows",
    )(sides, cross_ask, near_ask, far_ask, held)
    far = swapped(to_far, "yz", 1)
    cross = swapped(to_cross, "gx", 1)
    near = swapped(to_near, "yz", 0)

    left, right, *sums, lists, places = pl.pallas_call(
        early,
        out_shape=[LEFT, RIGHT] + SUMS + [jax.ShapeDtypeStruct((5, 128), jnp.int32), jax.ShapeDtypeStruct((10, 16), jnp.int32)],
        in_specs=[SMEM] * 4 + [HBM, VMEM, ANY, ANY, SMEM], out_specs=[VMEM] * 5 + [SMEM] * 2,
        scratch_shapes=[
            pltpu.VMEM((16, 64, 448), BF16), pltpu.VMEM((4, 64, 192), BF16),
            pltpu.SemaphoreType.DMA((8,)),
        ],
        compiler_params=params(), cost_estimate=cost(400000000, 6000000), name="early",
    )(
        sides, wanted, a_slot, p_cols, pltpu.with_memory_space_constraint(a_blocks, pltpu.HBM), held, chip, to_far, t_slot,
    )

    packed = jax.ShapeDtypeStruct((KC, HALF, 128), BF16)
    *outs, right, sum0, sum1, sum2 = pl.pallas_call(
        outward,
        out_shape=[packed] * 4 + [RIGHT] + SUMS,
        in_specs=[SMEM] * 3 + [VMEM] * 8, out_specs=[VMEM] * 8,
        input_output_aliases={4: 4, 5: 5, 6: 6, 7: 7},
        compiler_params=params(), cost_estimate=cost(400000000, 6000000), name="outward",
    )(places, t_slot, lists, left, right, *sums, cross, near, far)
    got = [
        swapped(outs[0], "gx", 0), swapped(outs[1], "gx", 1),
        swapped(outs[2], "yz", 0), swapped(outs[3], "yz", 1),
    ]

    own, *_ = pl.pallas_call(
        inward,
        out_shape=[jax.ShapeDtypeStruct((OWN * KC, HALF, 128), F32)] + SUMS,
        in_specs=[SMEM] * 3 + [VMEM] * 5, out_specs=[VMEM] * 4,
        input_output_aliases={5: 1, 6: 2, 7: 3},
        compiler_params=params(), cost_estimate=cost(1000000000, 8000000), name="inward",
    )(places, t_slot, lists, left, right, sum0, sum1, sum2)

    return pl.pallas_call(
        finish,
        out_shape=jax.ShapeDtypeStruct((OWN, 64, KC * 64), F32),
        in_specs=[VMEM] * 5, out_specs=VMEM,
        compiler_params=params(4), cost_estimate=cost(0, 1000000), name="finish",
    )(own, *got)


def solution(mesh):
    placed = (
        P(("gx", "yz"), None, None),
        P(("gx", "yz"), None, None),
        P(("gx", "yz"), None),
        P(("gx", "yz"), None, None),
        P(("gx", "yz"), None),
        P(("gx", "yz"), None, None, None),
    )
    return jax.shard_map(shards, mesh=mesh, in_specs=placed, out_specs=P(("gx", "yz"), None, None), check_vma=False)
```

time: 54.2 us -> 44.2 us (0.82)
  the two profiles are of different devices: /device:TPU:1 before, /device:TPU:4 now
where the time goes in v2:
time: 44.2 us; the launch traced here: 44.1 us
  starting transfers between devices  24.7 us (56%)
  Pallas kernels  16.9 us (38%)
  waiting for transfers between devices  2.26 us (5%)
    ppermute x11, starting transfers between devices, swapped(): return lax.ppermute(value, axis, pairs)  24.7 us
    pallas_call x1, Pallas kernels, shards(): pl.pallas_call(early, out_shape=[LEFT, RIGHT] + SUMS + [jax.ShapeDtypeStr...  7.34 us
    pallas_call x1, Pallas kernels, shards(): pl.pallas_call(inward, out_shape=[jax.ShapeDtypeStruct((OWN * KC, HALF, 1...  3.99 us
    pallas_call x1, Pallas kernels, shards(): pl.pallas_call(outward, out_shape=[packed] * 4 + [RIGHT] + SUMS, in_specs...  2.91 us
    ppermute x11, waiting for transfers between devices, swapped(): return lax.ppermute(value, axis, pairs)  2.26 us
    pallas_call x1, Pallas kernels, shards(): pl.pallas_call(fetch, out_shape=[jax.ShapeDtypeStruct(x.shape, x.dtype) f...  1.09 us
  transfers between devices with their start and end apart: 11, of which 2 were waited for; matrix products, arithmetic and copies ran while one was open for 0% of the time, Pallas kernels for 30%

profile of v2, /device:TPU:4, one launch (start us, length us, event | category | flops | bytes accessed | tf_op | source)
XLA Modules:
  0.0 44.1 jit_solution(3932932370858886517)
XLA Ops:
  0.0 0.0 collective-permute-start
  0.0 3.8 %collective-permute-start.1 = (s32[1,4,4]{2,1,0:T(4,128)}, s32[1,4,4]{2,1,0:T(4,128)S(1)}, u32[]{:S(2)}, u32[]{:S(2)}) collective-permute-start(s32[1,4,4]{2,1,0:T(4,128)} %refs_1_.1), channel_id=1, source_target_pairs={{16,32},{32,16},{48,64},{64,48},{80,96},{96,80},{112,128},{128,112... | collective-permute-start | bytes 200 | tf_op jit(solution)/shard_map/ppermute | solution.py:40
  3.8 2.2 %collective-permute-start.3 = (s32[1,4,4]{2,1,0:T(4,128)}, s32[1,4,4]{2,1,0:T(4,128)S(1)}, u32[]{:S(2)}, u32[]{:S(2)}) collective-permute-start(s32[1,4,4]{2,1,0:T(4,128)} %refs_1_.1), channel_id=1, source_target_pairs={{1,2},{2,1},{3,4},{4,3},{5,6},{6,5},{7,8},{8,7},{9,10},{10,9},{11,... | collective-permute-start | bytes 200 | tf_op jit(solution)/shard_map/ppermute | solution.py:40
  5.9 6.7 %collective-permute-start.2 = (s32[1,4,4]{2,1,0:T(4,128)}, s32[1,4,4]{2,1,0:T(4,128)S(1)}, u32[]{:S(2)}, u32[]{:S(2)}) collective-permute-start(s32[1,4,4]{2,1,0:T(4,128)} %refs_1_.1), channel_id=1, source_target_pairs={{0,1},{1,0},{2,3},{3,2},{4,5},{5,4},{6,7},{7,6},{8,9},{9,8},{10,11... | collective-permute-start | bytes 200 | tf_op jit(solution)/shard_map/ppermute | solution.py:40
  12.6 0.1 pad_add_fusion.sides
  12.7 1.1 %fetch.1 = (bf16[16,64,192]{2,1,0:T(8,128)(2,1)S(1)}, s32[1,4,4]{2,1,0:T(4,128)S(1)}, s32[7,16]{1,0:T(8,128)S(1)}, s32[3,16]{1,0:T(4,128)S(1)}, s32[3,3,7,16]{3,2,1,0:T(8,128)S(1)}) custom-call(bf16[16,64,192]{2,1,0:T(8,128)(2,1)} %refs_0_.1, s32[1,4,4]{2,1,0:T(4,128)} %refs_1_.1, s32[7,16]{1,0:T(8,128)} %bitcast.6, s32[3,16]{1,0:T(4,128)} %bitcast.7, ...), custom_call_target="tpu_custom_call" | custom-call | bytes 800000 | tf_op jit(solution)/shard_map/fetch/pallas_call | solution.py:231
  13.8 0.0 collective-permute-done.1.cross
  13.8 0.0 collective-permute-done.3.far
  13.8 0.6 %collective-permute-done.2.near = s32[1,4,4]{2,1,0:T(4,128)S(1)} collective-permute-done((s32[1,4,4]{2,1,0:T(4,128)}, s32[1,4,4]{2,1,0:T(4,128)S(1)}, u32[]{:S(2)}, u32[]{:S(2)}) %collective-permute-start.2) | collective-permute-done | bytes 96 | tf_op jit(solution)/shard_map/ppermute | solution.py:40
  14.4 0.7 %gather_rows.1 = (bf16[4,96,128]{2,1,0:T(8,128)(2,1)S(1)}, bf16[4,96,128]{2,1,0:T(8,128)(2,1)S(1)}, bf16[4,96,128]{2,1,0:T(8,128)(2,1)S(1)}) custom-call(s32[2]{0:T(128)S(1)} %pad_add_fusion.sides, s32[1,4,4]{2,1,0:T(4,128)S(1)} %collective-permute-done.1.cross, s32[1,4,4]{2,1,0:T(4,128)S(1)} %collective-permute-done.2.near, ...), custom_call_target="tpu_custom_call" | custom-call | bytes 700000 | tf_op jit(solution)/shard_map/gather_rows/pallas_call | solution.py:237
  15.1 0.1 collective-permute-start.4
  15.2 3.6 %collective-permute-start.5 = (bf16[4,96,128]{2,1,0:T(8,128)(2,1)S(1)}, bf16[4,96,128]{2,1,0:T(8,128)(2,1)S(1)}, u32[]{:S(2)}, u32[]{:S(2)}) collective-permute-start(bf16[4,96,128]{2,1,0:T(8,128)(2,1)S(1)} %get-tuple-element.43), channel_id=1, source_target_pairs={{0,1},{1,0},{2,3},{3,2},{4,5},{5,4},{6,7},{7,6},{8,9},{9,8},{10,11... | collective-permute-start | bytes 294920 | tf_op jit(solution)/shard_map/ppermute | solution.py:40
  18.8 0.0 collective-permute-start.6
  18.8 0.0 collective-permute-done.chip
  18.8 7.3 %early.1 = (bf16[128,96,128]{2,1,0:T(8,128)(2,1)S(1)}, bf16[32,3,128,128]{3,2,1,0:T(8,128)(2,1)S(1)}, f32[54,32,128]{2,1,0:T(8,128)S(1)}, f32[54,32,128]{2,1,0:T...) custom-call(s32[2]{0:T(128)S(1)} %pad_add_fusion.sides, ...), custom_call_target="tpu_custom_call" | custom-call | flops 400000000 | bytes 6000000 | tf_op jit(solution)/shard_map/early/pallas_call | solution.py:245
  26.2 0.0 collective-permute-done.4.cross
  26.2 0.0 collective-permute-done.5.near
  26.2 0.0 collective-permute-done.6.far
  26.2 2.9 %outward.1 = (bf16[9,32,128]{2,1,0:T(8,128)(2,1)S(1)}, bf16[9,32,128]{2,1,0:T(8,128)(2,1)S(1)}, bf16[9,32,128]{2,1,0:T(8,128)(2,1)S(1)}, bf16[9,32,128]{2,1,0:T(...) custom-call(s32[10,16]{1,0:T(8,128)S(1)} %get-tuple-element.35.place, ...), custom_call_target="tpu_custom_call", output_to_operand_aliasing={{4}: (4, {}), {5}: (5, {}), {6}: (6, {}), {7}: (7, {})} | custom-call | flops 400000000 | bytes 6000000 | tf_op jit(solution)/shard_map/outward/pallas_call | solution.py:259
  29.1 0.1 collective-permute-start.7
  29.2 4.2 %collective-permute-start.8 = (bf16[9,32,128]{2,1,0:T(8,128)(2,1)S(1)}, bf16[9,32,128]{2,1,0:T(8,128)(2,1)S(1)}, u32[]{:S(2)}, u32[]{:S(2)}) collective-permute-start(bf16[9,32,128]{2,1,0:T(8,128)(2,1)S(1)} %get-tuple-element.50), channel_id=1, source_target_pairs={{16,32},{32,16},{48,64},{64,48},{80,96},{96,80},{112,128},{128,112... | collective-permute-start | bytes 221192 | tf_op jit(solution)/shard_map/ppermute | solution.py:40
  33.4 3.1 %collective-permute-start.9 = (bf16[9,32,128]{2,1,0:T(8,128)(2,1)S(1)}, bf16[9,32,128]{2,1,0:T(8,128)(2,1)S(1)}, u32[]{:S(2)}, u32[]{:S(2)}) collective-permute-start(bf16[9,32,128]{2,1,0:T(8,128)(2,1)S(1)} %get-tuple-element.51), channel_id=1, source_target_pairs={{0,1},{1,0},{2,3},{3,2},{4,5},{5,4},{6,7},{7,6},{8,9},{9,8},{10,11... | collective-permute-start | bytes 221192 | tf_op jit(solution)/shard_map/ppermute | solution.py:40
  36.5 1.1 %collective-permute-start.10 = (bf16[9,32,128]{2,1,0:T(8,128)(2,1)S(1)}, bf16[9,32,128]{2,1,0:T(8,128)(2,1)S(1)}, u32[]{:S(2)}, u32[]{:S(2)}) collective-permute-start(bf16[9,32,128]{2,1,0:T(8,128)(2,1)S(1)} %get-tuple-element.52), channel_id=1, source_target_pairs={{1,2},{2,1},{3,4},{4,3},{5,6},{6,5},{7,8},{8,7},{9,10},{10,9},{11,... | collective-permute-start | bytes 221192 | tf_op jit(solution)/shard_map/ppermute | solution.py:40
  37.6 4.0 %inward.1 = (f32[18,32,128]{2,1,0:T(8,128)S(1)}, f32[54,32,128]{2,1,0:T(8,128)S(1)}, f32[54,32,128]{2,1,0:T(8,128)S(1)}, f32[54,32,128]{2,1,0:T(8,128)S(1)}) custom-call(s32[10,16]{1,0:T(8,128)S(1)} %get-tuple-element.35.places, s32[3,3,7,16]{3,2,1,0:T(8,128)S(1)} %get-tuple-element.34.t_slot, ...), custom_call_target="tpu_custom_call", output_to_operand_aliasing={{1}: (5, {}), {2}: (6, {}), {3}: (7, {})} | custom-call | flops 1000000000 | bytes 8000000 | tf_op jit(solution)/shard_map/inward/pallas_call | solution.py:271
  41.6 0.0 collective-permute-done.7.r0
  41.6 0.0 collective-permute-done.8.r1
  41.6 0.0 collective-permute-done.9.r2
  41.6 1.6 %collective-permute-done.10.r3 = bf16[9,32,128]{2,1,0:T(8,128)(2,1)S(1)} collective-permute-done((bf16[9,32,128]{2,1,0:T(8,128)(2,1)S(1)}, bf16[9,32,128]{2,1,0:T(8,128)(2,1)S(1)}, u32[]{:S(2)}, u32[]{:S(2)}) %collective-permute-start.10) | collective-permute-done | bytes 73760 | tf_op jit(solution)/shard_map/ppermute | solution.py:40
  43.2 0.9 %finish.1 = f32[2,64,576]{2,1,0:T(8,128)} custom-call(f32[18,32,128]{2,1,0:T(8,128)S(1)} %get-tuple-element.48.own, bf16[9,32,128]{2,1,0:T(8,128)(2,1)S(1)} %collective-permute-done.7.r0, bf16[9,32,128]{2,1,0:T(8,128)(2,1)S(1)} %collective-permute-done.8.r1, bf16[9,32,128]{2,1,0:T(8,128)(2,1)S(1)} %collective-permute-done.9.r2, ...), custom_call_target="tpu_custom_call" | custom-call | bytes 1000000 | tf_op jit(solution)/shard_map/finish/pallas_call | solution.py:279
Async XLA Ops:
  0.0 18.8 %collective-permute-start = (bf16[16,64,192]{2,1,0:T(8,128)(2,1)}, bf16[16,64,192]{2,1,0:T(8,128)(2,1)S(1)}, u32[]{:S(2)}, u32[]{:S(2)}) collective-permute-start(bf16[16,64,192]{2,1,0:T(8,128)(2,1)} %refs_0_.1), channel_id=1, source_target_pairs={{0,16},{16,0},{32,48},{48,32},{64,80},{80,64},{96,112},{112,96},{1... | collective-permute-start | bytes 1179656 | tf_op jit(solution)/shard_map/ppermute | solution.py:40
  0.0 13.8 %collective-permute-start.1 = (s32[1,4,4]{2,1,0:T(4,128)}, s32[1,4,4]{2,1,0:T(4,128)S(1)}, u32[]{:S(2)}, u32[]{:S(2)}) collective-permute-start(s32[1,4,4]{2,1,0:T(4,128)} %refs_1_.1), channel_id=1, source_target_pairs={{16,32},{32,16},{48,64},{64,48},{80,96},{96,80},{112,128},{128,112... | collective-permute-start | bytes 200 | tf_op jit(solution)/shard_map/ppermute | solution.py:40
  3.8 10.0 %collective-permute-start.3 = (s32[1,4,4]{2,1,0:T(4,128)}, s32[1,4,4]{2,1,0:T(4,128)S(1)}, u32[]{:S(2)}, u32[]{:S(2)}) collective-permute-start(s32[1,4,4]{2,1,0:T(4,128)} %refs_1_.1), channel_id=1, source_target_pairs={{1,2},{2,1},{3,4},{4,3},{5,6},{6,5},{7,8},{8,7},{9,10},{10,9},{11,... | collective-permute-start | bytes 200 | tf_op jit(solution)/shard_map/ppermute | solution.py:40
  5.9 8.5 %collective-permute-start.2 = (s32[1,4,4]{2,1,0:T(4,128)}, s32[1,4,4]{2,1,0:T(4,128)S(1)}, u32[]{:S(2)}, u32[]{:S(2)}) collective-permute-start(s32[1,4,4]{2,1,0:T(4,128)} %refs_1_.1), channel_id=1, source_target_pairs={{0,1},{1,0},{2,3},{3,2},{4,5},{5,4},{6,7},{7,6},{8,9},{9,8},{10,11... | collective-permute-start | bytes 200 | tf_op jit(solution)/shard_map/ppermute | solution.py:40
  15.1 11.0 %collective-permute-start.4 = (bf16[4,96,128]{2,1,0:T(8,128)(2,1)S(1)}, bf16[4,96,128]{2,1,0:T(8,128)(2,1)S(1)}, u32[]{:S(2)}, u32[]{:S(2)}) collective-permute-start(bf16[4,96,128]{2,1,0:T(8,128)(2,1)S(1)} %get-tuple-element.42), channel_id=1, source_target_pairs={{16,32},{32,16},{48,64},{64,48},{80,96},{96,80},{112,128},{128,112... | collective-permute-start | bytes 294920 | tf_op jit(solution)/shard_map/ppermute | solution.py:40
  15.2 10.9 %collective-permute-start.5 = (bf16[4,96,128]{2,1,0:T(8,128)(2,1)S(1)}, bf16[4,96,128]{2,1,0:T(8,128)(2,1)S(1)}, u32[]{:S(2)}, u32[]{:S(2)}) collective-permute-start(bf16[4,96,128]{2,1,0:T(8,128)(2,1)S(1)} %get-tuple-element.43), channel_id=1, source_target_pairs={{0,1},{1,0},{2,3},{3,2},{4,5},{5,4},{6,7},{7,6},{8,9},{9,8},{10,11... | collective-permute-start | bytes 294920 | tf_op jit(solution)/shard_map/ppermute | solution.py:40
  18.8 7.4 %collective-permute-start.6 = (bf16[4,96,128]{2,1,0:T(8,128)(2,1)S(1)}, bf16[4,96,128]{2,1,0:T(8,128)(2,1)S(1)}, u32[]{:S(2)}, u32[]{:S(2)}) collective-permute-start(bf16[4,96,128]{2,1,0:T(8,128)(2,1)S(1)} %get-tuple-element.33.after), channel_id=1, source_target_pairs={{1,2},{2,1},{3,4},{4,3},{5,6},{6,5},{7,8},{8,7},{9,10},{10,9},{11,... | collective-permute-start | bytes 294920 | tf_op jit(solution)/shard_map/ppermute | solution.py:40
  29.1 12.5 %collective-permute-start.7 = (bf16[9,32,128]{2,1,0:T(8,128)(2,1)S(1)}, bf16[9,32,128]{2,1,0:T(8,128)(2,1)S(1)}, u32[]{:S(2)}, u32[]{:S(2)}) collective-permute-start(bf16[9,32,128]{2,1,0:T(8,128)(2,1)S(1)} %get-tuple-element.49), channel_id=1, source_target_pairs={{0,16},{16,0},{32,48},{48,32},{64,80},{80,64},{96,112},{112,96},{1... | collective-permute-start | bytes 221192 | tf_op jit(solution)/shard_map/ppermute | solution.py:40
  29.2 12.4 %collective-permute-start.8 = (bf16[9,32,128]{2,1,0:T(8,128)(2,1)S(1)}, bf16[9,32,128]{2,1,0:T(8,128)(2,1)S(1)}, u32[]{:S(2)}, u32[]{:S(2)}) collective-permute-start(bf16[9,32,128]{2,1,0:T(8,128)(2,1)S(1)} %get-tuple-element.50), channel_id=1, source_target_pairs={{16,32},{32,16},{48,64},{64,48},{80,96},{96,80},{112,128},{128,112... | collective-permute-start | bytes 221192 | tf_op jit(solution)/shard_map/ppermute | solution.py:40
  33.4 8.2 %collective-permute-start.9 = (bf16[9,32,128]{2,1,0:T(8,128)(2,1)S(1)}, bf16[9,32,128]{2,1,0:T(8,128)(2,1)S(1)}, u32[]{:S(2)}, u32[]{:S(2)}) collective-permute-start(bf16[9,32,128]{2,1,0:T(8,128)(2,1)S(1)} %get-tuple-element.51), channel_id=1, source_target_pairs={{0,1},{1,0},{2,3},{3,2},{4,5},{5,4},{6,7},{7,6},{8,9},{9,8},{10,11... | collective-permute-start | bytes 221192 | tf_op jit(solution)/shard_map/ppermute | solution.py:40
  36.5 6.8 %collective-permute-start.10 = (bf16[9,32,128]{2,1,0:T(8,128)(2,1)S(1)}, bf16[9,32,128]{2,1,0:T(8,128)(2,1)S(1)}, u32[]{:S(2)}, u32[]{:S(2)}) collective-permute-start(bf16[9,32,128]{2,1,0:T(8,128)(2,1)S(1)} %get-tuple-element.52), channel_id=1, source_target_pairs={{1,2},{2,1},{3,4},{4,3},{5,6},{6,5},{7,8},{8,7},{9,10},{10,9},{11,... | collective-permute-start | bytes 221192 | tf_op jit(solution)/shard_map/ppermute | solution.py:40

commit v3 on v2

--- a/solution.py
+++ b/solution.py
@@ -18,7 +18,8 @@
 HBM = pl.BlockSpec(memory_space=pltpu.HBM)
 GROUP = 14
 AHEAD = 2
-LEFT = jax.ShapeDtypeStruct((128, 96, 128), BF16)
+I32 = jnp.int32
+LEFT = jax.ShapeDtypeStruct((112, 96, 128), BF16)
 RIGHT = jax.ShapeDtypeStruct((32, 3, 128, 128), BF16)
 SUMS = [jax.ShapeDtypeStruct((BINS, HALF, 128), F32)] * 3
 
@@ -81,43 +82,76 @@
     spread(rows[:, 0:128], last, right, index)
 
 
-def add_pairs(pairs, places, t_slot, left, right, sums):
+def add_pairs(pairs, bins, slots, left, right, sums):
     for pair in pairs:
-        i, a = pair >> 3, pair & 7
-        slot = places[a, i]
+        i, a = pair & 15, pair >> 4
+        slot = slots[a, i]
         wide = jnp.concatenate([right[slot, p] for p in range(3)], axis=1)
         value = jnp.dot(left[pair], wide, preferred_element_type=F32)
         for q in range(3):
-            first = places[7 + q, i]
             for p in range(3):
-                where = first + t_slot[q, p, a, i]
+                where = bins[q, p, a, i]
                 sums[p][where] = sums[p][where] + value[q * HALF : (q + 1) * HALF, p * 128 : (p + 1) * 128]
 
 
-def later_pairs(lists, b):
-    sent_far, shift_sent, going, kept_far, shift_kept = (lists[4, n] for n in range(5))
-    pairs = []
-    for j in range(GROUP):
-        k = b * GROUP + j
-        m = k - going
-        row = jnp.where(k < sent_far, 2, jnp.where(m < 0, 0, jnp.where(m < kept_far, 3, 1)))
-        near = jnp.where(k < sent_far, k, k + shift_sent)
-        column = jnp.where(m < 0, near, jnp.where(m < kept_far, m, m + shift_kept))
-        pairs.append(lists[row, column])
-    return pairs
+def arrange(sides, a_slot, p_cols, t_slot, order, bins, slots):
+    flip_g, flip_y = 4 * (1 - sides[0]), 4 * (1 - sides[1])
+    slot, aim = a_slot[...], p_cols[...]
+    slots[...] = jnp.where(slot < 16, slot, slot ^ jnp.where(slot < 24, flip_g, flip_y))
+    side = ((aim >> 1) - 1) << 2
+    side = (side ^ jnp.where(side < 8, flip_g, flip_y)) >> 2
+    target = KC * jnp.where(aim < OWN, aim, OWN + side)
+    for q in range(3):
+        for p in range(3):
+            bins[q, p] = t_slot[q, p] + target[q : q + 1]
+
+    top = jnp.maximum(jnp.maximum(aim[0:1], aim[1:2]), aim[2:3])
+    unused = jnp.full((1, 16), 1000, I32)
+    flat = jnp.concatenate([slot[a : a + 1] for a in range(7)] + [unused], axis=1)
+    tops = jnp.concatenate([top] * 8, axis=1)
+    real, own, sent = flat < 1000, flat < 16, tops >= OWN
+    one = lambda mask: jnp.where(mask, 1.0, 0.0).astype(F32)
+    kinds = [one(own & sent), one(own & ~sent), one(real & ~own & sent), one(real & ~own & ~sent)]
+    kinds = jnp.concatenate(kinds + [jnp.zeros((4, 128), F32)], axis=0).astype(BF16)
+    down = lax.broadcasted_iota(I32, (128, 128), 0)
+    across = lax.broadcasted_iota(I32, (128, 128), 1)
+    before = jnp.where(down < across, 1.0, 0.0).astype(BF16)
+    rank = jnp.dot(kinds, before, preferred_element_type=F32)
+    total = jnp.dot(kinds, jnp.ones((128, 128), BF16), preferred_element_type=F32)
+    n0, n1, n2, n3 = total[0:1], total[1:2], total[2:3], total[3:4]
+    done = jnp.minimum(jnp.floor((n0 + n1) * (1.0 / GROUP) + 0.25 / GROUP), AHEAD) * GROUP
+    head = jnp.minimum(n0, done)
+    tail = done - head
+    going = done + n2 + n0 - head
+    r0, r1, r2, r3 = rank[0:1], rank[1:2], rank[2:3], rank[3:4]
+    place = jnp.where(r0 < head, r0, done + n2 + r0 - head) * kinds[0:1].astype(F32)
+    place = place + jnp.where(r1 < tail, head + r1, going + n3 + r1 - tail) * kinds[1:2].astype(F32)
+    place = place + (done + r2) * kinds[2:3].astype(F32) + (going + r3) * kinds[3:4].astype(F32)
+    place = jnp.where(real, place.astype(I32), across[0:1])
+    hit = jnp.where(down == place, 1.0, 0.0).astype(BF16)
+    names = across[0:8].astype(F32).astype(BF16)
+    found = lax.dot_general(names, hit, (((1,), (1,)), ((), ())), preferred_element_type=F32)
+    rows = lax.broadcasted_iota(I32, (8, 128), 0)
+    order[...] = jnp.where(rows == 0, found, jnp.where(rows == 1, done, going)).astype(I32)
 
 
 def early(
     sides, wanted, a_slot, p_cols, a_blocks, p_blocks, chip, after, t_slot,
-    left, right, sum0, sum1, sum2, lists, places, held, rows4, sems,
+    left, right, sum0, sum1, sum2, order, bins, slots, held, rows4, order_s, bins_s, slots_s, sems,
 ):
     sums = (sum0, sum1, sum2)
     row = 1 - sides[0]
-    flip_g, flip_y = 4 * (1 - sides[0]), 4 * (1 - sides[1])
     loads = [pltpu.make_async_copy(a_blocks.at[pl.ds(4 * c, 4)], held.at[pl.ds(4 * c, 4)], sems.at[c]) for c in range(4)]
     pulls = [pltpu.make_async_copy(chip.at[wanted[0, row, h]], rows4.at[h], sems.at[4 + h]) for h in range(4)]
     for copy in loads + pulls:
         copy.start()
+    arrange(sides, a_slot, p_cols, t_slot, order, bins, slots)
+    tables = [
+        pltpu.make_async_copy(source, out, sems.at[8 + n])
+        for n, (source, out) in enumerate(((order, order_s), (bins, bins_s), (slots, slots_s)))
+    ]
+    for copy in tables:
+        copy.start()
 
     def clear(j, carry):
         for total in sums:
@@ -125,7 +159,6 @@
         return carry
 
     lax.fori_loop(0, BINS, clear, 0)
-    counts = [jnp.int32(0)] * 4
     for c in range(4):
         loads[c].wait()
         for i in range(4 * c, 4 * c + 4):
@@ -134,75 +167,43 @@
             full = lax.dot_general(rows, held[i], (((0,), (0,)), ((), ())), preferred_element_type=F32).astype(BF16)
             top = jnp.concatenate([full[q * 64 : q * 64 + 32] for q in range(3)], axis=0)
             bottom = jnp.concatenate([full[q * 64 + 32 : q * 64 + 64] for q in range(3)], axis=0)
-            for q in range(3):
-                aim = p_cols[q, i]
-                side = ((aim >> 1) - 1) << 2
-                side = (side ^ jnp.where(side < 8, flip_g, flip_y)) >> 2
-                places[7 + q, i] = KC * jnp.where(aim < OWN, aim, OWN + side)
-            sent = jnp.maximum(jnp.maximum(places[7, i], places[8, i]), places[9, i]) >= OWN * KC
             for a in range(7):
-                pair = i * 8 + a
-                left[pair] = jnp.concatenate([top[:, a * 64 : (a + 1) * 64], bottom[:, a * 64 : (a + 1) * 64]], axis=1)
-                slot = a_slot[a, i]
-                own = slot < 16
-                places[a, i] = jnp.where(own, slot, slot ^ jnp.where(slot < 24, flip_g, flip_y))
-                for kind, here in enumerate((own & sent, own & ~sent, ~own & sent, ~own & ~sent)):
-                    lists[kind, counts[kind]] = pair
-                    counts[kind] = counts[kind] + jnp.where(here, 1, 0)
-    groups = jnp.minimum((counts[0] + counts[1]) // GROUP, AHEAD)
-    done = groups * GROUP
-    lists[4, 0] = counts[2]
-    lists[4, 1] = jnp.minimum(done, counts[0]) - counts[2]
-    lists[4, 2] = counts[2] + counts[0] - jnp.minimum(done, counts[0])
-    lists[4, 3] = counts[3]
-    lists[4, 4] = jnp.maximum(done - counts[0], 0) - counts[3]
-    lists[4, 5] = 112 // GROUP - groups
-    first = counts[0]
-    for h in range(4):
-        pulls[h].wait()
+                left[a * 16 + i] = jnp.concatenate([top[:, a * 64 : (a + 1) * 64], bottom[:, a * 64 : (a + 1) * 64]], axis=1)
+    for copy in pulls + tables:
+        copy.wait()
     for h in range(4):
         spread_rows(rows4[h], right, 16 + h)
 
     def body(b, carry):
-        pairs = []
-        for j in range(GROUP):
-            k = b * GROUP + j
-            head = k < first
-            pairs.append(lists[jnp.where(head, 0, 1), jnp.where(head, k, k - first)])
-        add_pairs(pairs, places, t_slot, left, right, sums)
-        return carry
-
-    lax.fori_loop(0, groups, body, 0)
+        add_pairs([order_s[0, b * GROUP + j] for j in range(GROUP)], bins_s, slots_s, left, right, sums)
+        return carry
+
+    lax.fori_loop(0, order_s[1, 0] // GROUP, body, 0)
 
 
 def outward(
-    places, t_slot, lists, left, right_in, s0, s1, s2, cross, near, far, o0, o1, o2, o3, right, sum0, sum1, sum2
+    bins, slots, order, left, right_in, s0, s1, s2, cross, near, far, o0, o1, o2, o3, right, sum0, sum1, sum2
 ):
     for h in range(4):
         for rows, base in ((cross, 20), (near, 24), (far, 28)):
             spread(rows[h, 0:64], rows[h, 64:96], right, base + h)
-    going = lists[4, 2]
 
     def body(b, carry):
-        pairs = later_pairs(lists, b)
-        add_pairs(pairs, places, t_slot, left, right, (sum0, sum1, sum2))
-        return carry
-
-    lax.fori_loop(0, (going + GROUP - 1) // GROUP, body, 0)
+        add_pairs([order[0, b * GROUP + j] for j in range(GROUP)], bins, slots, left, right, (sum0, sum1, sum2))
+        return carry
+
+    lax.fori_loop(order[1, 0] // GROUP, (order[2, 0] + GROUP - 1) // GROUP, body, 0)
     for k, out in enumerate((o0, o1, o2, o3)):
         part = pl.ds((OWN + k) * KC, KC)
         out[...] = (sum0[part] + sum1[part] + sum2[part]).astype(BF16)
 
 
-def inward(places, t_slot, lists, left, right, s0, s1, s2, out, sum0, sum1, sum2):
-    going = lists[4, 2]
-
+def inward(bins, slots, order, left, right, s0, s1, s2, out, sum0, sum1, sum2):
     def body(b, carry):
-        pairs = later_pairs(lists, b)
-        add_pairs(pairs, places, t_slot, left, right, (sum0, sum1, sum2))
-        return carry
-
-    lax.fori_loop((going + GROUP - 1) // GROUP, lists[4, 5], body, 0)
+        add_pairs([order[0, b * GROUP + j] for j in range(GROUP)], bins, slots, left, right, (sum0, sum1, sum2))
+        return carry
+
+    lax.fori_loop((order[2, 0] + GROUP - 1) // GROUP, 112 // GROUP, body, 0)
     part = pl.ds(0, OWN * KC)
     out[...] = sum0[part] + sum1[part] + sum2[part]
 
@@ -242,13 +243,15 @@
     cross = swapped(to_cross, "gx", 1)
     near = swapped(to_near, "yz", 0)
 
-    left, right, *sums, lists, places = pl.pallas_call(
+    left, right, *sums, order, bins, slots = pl.pallas_call(
         early,
-        out_shape=[LEFT, RIGHT] + SUMS + [jax.ShapeDtypeStruct((5, 128), jnp.int32), jax.ShapeDtypeStruct((10, 16), jnp.int32)],
-        in_specs=[SMEM] * 4 + [HBM, VMEM, ANY, ANY, SMEM], out_specs=[VMEM] * 5 + [SMEM] * 2,
+        out_shape=[LEFT, RIGHT] + SUMS + [
+            jax.ShapeDtypeStruct((8, 128), I32), jax.ShapeDtypeStruct((3, 3, 7, 16), I32), jax.ShapeDtypeStruct((7, 16), I32),
+        ],
+        in_specs=[SMEM] * 2 + [VMEM] * 2 + [HBM, VMEM, ANY, ANY, VMEM], out_specs=[VMEM] * 8,
         scratch_shapes=[
             pltpu.VMEM((16, 64, 448), BF16), pltpu.VMEM((4, 64, 192), BF16),
-            pltpu.SemaphoreType.DMA((8,)),
+            pltpu.SMEM((8, 128), I32), pltpu.SMEM((3, 3, 7, 16), I32), pltpu.SMEM((7, 16), I32), pltpu.SemaphoreType.DMA((11,)),
         ],
         compiler_params=params(), cost_estimate=cost(400000000, 6000000), name="early",
     )(
@@ -262,7 +265,7 @@
         in_specs=[SMEM] * 3 + [VMEM] * 8, out_specs=[VMEM] * 8,
         input_output_aliases={4: 4, 5: 5, 6: 6, 7: 7},
         compiler_params=params(), cost_estimate=cost(400000000, 6000000), name="outward",
-    )(places, t_slot, lists, left, right, *sums, cross, near, far)
+    )(bins, slots, order, left, right, *sums, cross, near, far)
     got = [
         swapped(outs[0], "gx", 0), swapped(outs[1], "gx", 1),
         swapped(outs[2], "yz", 0), swapped(outs[3], "yz", 1),
@@ -274,7 +277,7 @@
         in_specs=[SMEM] * 3 + [VMEM] * 5, out_specs=[VMEM] * 4,
         input_output_aliases={5: 1, 6: 2, 7: 3},
         compiler_params=params(), cost_estimate=cost(1000000000, 8000000), name="inward",
-    )(places, t_slot, lists, left, right, sum0, sum1, sum2)
+    )(bins, slots, order, left, right, sum0, sum1, sum2)
 
     return pl.pallas_call(
         finish,

time: 44.2 us -> 41.7 us (0.943)
  the two profiles are of different devices: /device:TPU:4 before, /device:TPU:0 now
where the time goes in v3:
time: 41.7 us; the launch traced here: 41.6 us
  starting transfers between devices  22.3 us (53%)
  Pallas kernels  13.7 us (33%)
  waiting for transfers between devices  5.43 us (13%)
    ppermute x11, starting transfers between devices, swapped(): return lax.ppermute(value, axis, pairs)  22.3 us
    ppermute x11, waiting for transfers between devices, swapped(): return lax.ppermute(value, axis, pairs)  5.43 us
    pallas_call x1, Pallas kernels, shards(): pl.pallas_call(early, out_shape=[LEFT, RIGHT] + SUMS + [jax.ShapeDtypeStr...  5.24 us
    pallas_call x1, Pallas kernels, shards(): pl.pallas_call(inward, out_shape=[jax.ShapeDtypeStruct((OWN * KC, HALF, 1...  3.22 us
    pallas_call x1, Pallas kernels, shards(): pl.pallas_call(outward, out_shape=[packed] * 4 + [RIGHT] + SUMS, in_specs...  2.48 us
    pallas_call x1, Pallas kernels, shards(): pl.pallas_call(fetch, out_shape=[jax.ShapeDtypeStruct(x.shape, x.dtype) f...  1.09 us
    pallas_call x1, Pallas kernels, shards(): pl.pallas_call(finish, out_shape=jax.ShapeDtypeStruct((OWN, 64, KC * 64),...  0.88 us
  transfers between devices with their start and end apart: 11, of which 3 were waited for; matrix products, arithmetic and copies ran while one was open for 0% of the time, Pallas kernels for 25%

profile of v3, /device:TPU:0, one launch (start us, length us, event | category | flops | bytes accessed | tf_op | source)
XLA Modules:
  0.0 41.6 jit_solution(15604607307117353311)
XLA Ops:
  0.0 0.0 collective-permute-start
  0.0 2.3 %collective-permute-start.1 = (s32[1,4,4]{2,1,0:T(4,128)}, s32[1,4,4]{2,1,0:T(4,128)S(1)}, u32[]{:S(2)}, u32[]{:S(2)}) collective-permute-start(s32[1,4,4]{2,1,0:T(4,128)} %refs_1_.1), channel_id=1, source_target_pairs={{16,32},{32,16},{48,64},{64,48},{80,96},{96,80},{112,128},{128,112... | collective-permute-start | bytes 200 | tf_op jit(solution)/shard_map/ppermute | solution.py:41
  2.4 8.0 %collective-permute-start.3 = (s32[1,4,4]{2,1,0:T(4,128)}, s32[1,4,4]{2,1,0:T(4,128)S(1)}, u32[]{:S(2)}, u32[]{:S(2)}) collective-permute-start(s32[1,4,4]{2,1,0:T(4,128)} %refs_1_.1), channel_id=1, source_target_pairs={{1,2},{2,1},{3,4},{4,3},{5,6},{6,5},{7,8},{8,7},{9,10},{10,9},{11,... | collective-permute-start | bytes 200 | tf_op jit(solution)/shard_map/ppermute | solution.py:41
  10.4 0.0 collective-permute-start.2
  10.4 0.1 pad_add_fusion.sides
  10.5 1.1 %fetch.1 = (bf16[16,64,192]{2,1,0:T(8,128)(2,1)S(1)}, s32[1,4,4]{2,1,0:T(4,128)S(1)}, s32[7,16]{1,0:T(8,128)S(1)}, s32[3,16]{1,0:T(4,128)S(1)}, s32[3,3,7,16]{3,2,1,0:T(8,128)S(1)}) custom-call(bf16[16,64,192]{2,1,0:T(8,128)(2,1)} %refs_0_.1, s32[1,4,4]{2,1,0:T(4,128)} %refs_1_.1, s32[7,16]{1,0:T(8,128)} %bitcast.6, s32[3,16]{1,0:T(4,128)} %bitcast.7, ...), custom_call_target="tpu_custom_call" | custom-call | bytes 800000 | tf_op jit(solution)/shard_map/fetch/pallas_call | solution.py:232
  11.6 0.0 collective-permute-done.1.cross
  11.6 0.6 %collective-permute-done.3.far = s32[1,4,4]{2,1,0:T(4,128)S(1)} collective-permute-done((s32[1,4,4]{2,1,0:T(4,128)}, s32[1,4,4]{2,1,0:T(4,128)S(1)}, u32[]{:S(2)}, u32[]{:S(2)}) %collective-permute-start.3) | collective-permute-done | bytes 96 | tf_op jit(solution)/shard_map/ppermute | solution.py:41
  12.2 3.5 %collective-permute-done.2.near = s32[1,4,4]{2,1,0:T(4,128)S(1)} collective-permute-done((s32[1,4,4]{2,1,0:T(4,128)}, s32[1,4,4]{2,1,0:T(4,128)S(1)}, u32[]{:S(2)}, u32[]{:S(2)}) %collective-permute-start.2) | collective-permute-done | bytes 96 | tf_op jit(solution)/shard_map/ppermute | solution.py:41
  15.7 0.7 %gather_rows.1 = (bf16[4,96,128]{2,1,0:T(8,128)(2,1)S(1)}, bf16[4,96,128]{2,1,0:T(8,128)(2,1)S(1)}, bf16[4,96,128]{2,1,0:T(8,128)(2,1)S(1)}) custom-call(s32[2]{0:T(128)S(1)} %pad_add_fusion.sides, s32[1,4,4]{2,1,0:T(4,128)S(1)} %collective-permute-done.1.cross, s32[1,4,4]{2,1,0:T(4,128)S(1)} %collective-permute-done.2.near, ...), custom_call_target="tpu_custom_call" | custom-call | bytes 700000 | tf_op jit(solution)/shard_map/gather_rows/pallas_call | solution.py:238
  16.4 0.1 collective-permute-start.4
  16.5 0.1 collective-permute-start.5
  16.6 3.9 %collective-permute-start.6 = (bf16[4,96,128]{2,1,0:T(8,128)(2,1)S(1)}, bf16[4,96,128]{2,1,0:T(8,128)(2,1)S(1)}, u32[]{:S(2)}, u32[]{:S(2)}) collective-permute-start(bf16[4,96,128]{2,1,0:T(8,128)(2,1)S(1)} %get-tuple-element.34.after), channel_id=1, source_target_pairs={{1,2},{2,1},{3,4},{4,3},{5,6},{6,5},{7,8},{8,7},{9,10},{10,9},{11,... | collective-permute-start | bytes 294920 | tf_op jit(solution)/shard_map/ppermute | solution.py:41
  20.6 0.0 collective-permute-done.chip
  20.6 5.2 %early.1 = (bf16[112,96,128]{2,1,0:T(8,128)(2,1)S(1)}, bf16[32,3,128,128]{3,2,1,0:T(8,128)(2,1)S(1)}, f32[54,32,128]{2,1,0:T(8,128)S(1)}, f32[54,32,128]{2,1,0:T...) custom-call(s32[2]{0:T(128)S(1)} %pad_add_fusion.sides, ...), custom_call_target="tpu_custom_call" | custom-call | flops 400000000 | bytes 6000000 | tf_op jit(solution)/shard_map/early/pallas_call | solution.py:246
  25.8 0.0 collective-permute-done.4.cross
  25.8 0.0 collective-permute-done.5.near
  25.9 0.0 collective-permute-done.6.far
  25.9 2.5 %outward.1 = (bf16[9,32,128]{2,1,0:T(8,128)(2,1)S(1)}, bf16[9,32,128]{2,1,0:T(8,128)(2,1)S(1)}, bf16[9,32,128]{2,1,0:T(8,128)(2,1)S(1)}, bf16[9,32,128]{2,1,0:T(...) custom-call(s32[3,3,7,16]{3,2,1,0:T(8,128)S(1)} %get-tuple-element.3, ...), custom_call_target="tpu_custom_call", output_to_operand_aliasing={{4}: (4, {}), {5}: (5, {}), {6}: (6, {}), {7}: (7, {})} | custom-call | flops 400000000 | bytes 6000000 | tf_op jit(solution)/shard_map/outward/pallas_call | solution.py:262
  28.4 0.1 collective-permute-start.7
  28.5 3.3 %collective-permute-start.8 = (bf16[9,32,128]{2,1,0:T(8,128)(2,1)S(1)}, bf16[9,32,128]{2,1,0:T(8,128)(2,1)S(1)}, u32[]{:S(2)}, u32[]{:S(2)}) collective-permute-start(bf16[9,32,128]{2,1,0:T(8,128)(2,1)S(1)} %get-tuple-element.52), channel_id=1, source_target_pairs={{16,32},{32,16},{48,64},{64,48},{80,96},{96,80},{112,128},{128,112... | collective-permute-start | bytes 221192 | tf_op jit(solution)/shard_map/ppermute | solution.py:41
  31.7 1.0 %collective-permute-start.9 = (bf16[9,32,128]{2,1,0:T(8,128)(2,1)S(1)}, bf16[9,32,128]{2,1,0:T(8,128)(2,1)S(1)}, u32[]{:S(2)}, u32[]{:S(2)}) collective-permute-start(bf16[9,32,128]{2,1,0:T(8,128)(2,1)S(1)} %get-tuple-element.53), channel_id=1, source_target_pairs={{0,1},{1,0},{2,3},{3,2},{4,5},{5,4},{6,7},{7,6},{8,9},{9,8},{10,11... | collective-permute-start | bytes 221192 | tf_op jit(solution)/shard_map/ppermute | solution.py:41
  32.7 3.4 %collective-permute-start.10 = (bf16[9,32,128]{2,1,0:T(8,128)(2,1)S(1)}, bf16[9,32,128]{2,1,0:T(8,128)(2,1)S(1)}, u32[]{:S(2)}, u32[]{:S(2)}) collective-permute-start(bf16[9,32,128]{2,1,0:T(8,128)(2,1)S(1)} %get-tuple-element.54), channel_id=1, source_target_pairs={{1,2},{2,1},{3,4},{4,3},{5,6},{6,5},{7,8},{8,7},{9,10},{10,9},{11,... | collective-permute-start | bytes 221192 | tf_op jit(solution)/shard_map/ppermute | solution.py:41
  36.2 3.2 %inward.1 = (f32[18,32,128]{2,1,0:T(8,128)S(1)}, f32[54,32,128]{2,1,0:T(8,128)S(1)}, f32[54,32,128]{2,1,0:T(8,128)S(1)}, f32[54,32,128]{2,1,0:T(8,128)S(1)}) custom-call(s32[3,3,7,16]{3,2,1,0:T(8,128)S(1)} %get-tuple-element.36.bins, s32[7,16]{1,0:T(8,128)S(1)} %get-tuple-element.37.slots, ...), custom_call_target="tpu_custom_call", output_to_operand_aliasing={{1}: (5, {}), {2}: (6, {}), {3}: (7, {})} | custom-call | flops 1000000000 | bytes 8000000 | tf_op jit(solution)/shard_map/inward/pallas_call | solution.py:274
  39.4 0.0 collective-permute-done.7.r0
  39.4 0.0 collective-permute-done.8.r1
  39.4 0.0 collective-permute-done.9.r2
  39.4 1.3 %collective-permute-done.10.r3 = bf16[9,32,128]{2,1,0:T(8,128)(2,1)S(1)} collective-permute-done((bf16[9,32,128]{2,1,0:T(8,128)(2,1)S(1)}, bf16[9,32,128]{2,1,0:T(8,128)(2,1)S(1)}, u32[]{:S(2)}, u32[]{:S(2)}) %collective-permute-start.10) | collective-permute-done | bytes 73760 | tf_op jit(solution)/shard_map/ppermute | solution.py:41
  40.7 0.9 %finish.1 = f32[2,64,576]{2,1,0:T(8,128)} custom-call(f32[18,32,128]{2,1,0:T(8,128)S(1)} %get-tuple-element.50.own, bf16[9,32,128]{2,1,0:T(8,128)(2,1)S(1)} %collective-permute-done.7.r0, bf16[9,32,128]{2,1,0:T(8,128)(2,1)S(1)} %collective-permute-done.8.r1, bf16[9,32,128]{2,1,0:T(8,128)(2,1)S(1)} %collective-permute-done.9.r2, ...), custom_call_target="tpu_custom_call" | custom-call | bytes 1000000 | tf_op jit(solution)/shard_map/finish/pallas_call | solution.py:282
Async XLA Ops:
  0.0 20.6 %collective-permute-start = (bf16[16,64,192]{2,1,0:T(8,128)(2,1)}, bf16[16,64,192]{2,1,0:T(8,128)(2,1)S(1)}, u32[]{:S(2)}, u32[]{:S(2)}) collective-permute-start(bf16[16,64,192]{2,1,0:T(8,128)(2,1)} %refs_0_.1), channel_id=1, source_target_pairs={{0,16},{16,0},{32,48},{48,32},{64,80},{80,64},{96,112},{112,96},{1... | collective-permute-start | bytes 1179656 | tf_op jit(solution)/shard_map/ppermute | solution.py:41
  0.0 11.6 %collective-permute-start.1 = (s32[1,4,4]{2,1,0:T(4,128)}, s32[1,4,4]{2,1,0:T(4,128)S(1)}, u32[]{:S(2)}, u32[]{:S(2)}) collective-permute-start(s32[1,4,4]{2,1,0:T(4,128)} %refs_1_.1), channel_id=1, source_target_pairs={{16,32},{32,16},{48,64},{64,48},{80,96},{96,80},{112,128},{128,112... | collective-permute-start | bytes 200 | tf_op jit(solution)/shard_map/ppermute | solution.py:41
  2.4 9.8 %collective-permute-start.3 = (s32[1,4,4]{2,1,0:T(4,128)}, s32[1,4,4]{2,1,0:T(4,128)S(1)}, u32[]{:S(2)}, u32[]{:S(2)}) collective-permute-start(s32[1,4,4]{2,1,0:T(4,128)} %refs_1_.1), channel_id=1, source_target_pairs={{1,2},{2,1},{3,4},{4,3},{5,6},{6,5},{7,8},{8,7},{9,10},{10,9},{11,... | collective-permute-start | bytes 200 | tf_op jit(solution)/shard_map/ppermute | solution.py:41
  10.4 5.3 %collective-permute-start.2 = (s32[1,4,4]{2,1,0:T(4,128)}, s32[1,4,4]{2,1,0:T(4,128)S(1)}, u32[]{:S(2)}, u32[]{:S(2)}) collective-permute-start(s32[1,4,4]{2,1,0:T(4,128)} %refs_1_.1), channel_id=1, source_target_pairs={{0,1},{1,0},{2,3},{3,2},{4,5},{5,4},{6,7},{7,6},{8,9},{9,8},{10,11... | collective-permute-start | bytes 200 | tf_op jit(solution)/shard_map/ppermute | solution.py:41
  16.4 9.4 %collective-permute-start.4 = (bf16[4,96,128]{2,1,0:T(8,128)(2,1)S(1)}, bf16[4,96,128]{2,1,0:T(8,128)(2,1)S(1)}, u32[]{:S(2)}, u32[]{:S(2)}) collective-permute-start(bf16[4,96,128]{2,1,0:T(8,128)(2,1)S(1)} %get-tuple-element.44), channel_id=1, source_target_pairs={{16,32},{32,16},{48,64},{64,48},{80,96},{96,80},{112,128},{128,112... | collective-permute-start | bytes 294920 | tf_op jit(solution)/shard_map/ppermute | solution.py:41
  16.5 9.3 %collective-permute-start.5 = (bf16[4,96,128]{2,1,0:T(8,128)(2,1)S(1)}, bf16[4,96,128]{2,1,0:T(8,128)(2,1)S(1)}, u32[]{:S(2)}, u32[]{:S(2)}) collective-permute-start(bf16[4,96,128]{2,1,0:T(8,128)(2,1)S(1)} %get-tuple-element.45), channel_id=1, source_target_pairs={{0,1},{1,0},{2,3},{3,2},{4,5},{5,4},{6,7},{7,6},{8,9},{9,8},{10,11... | collective-permute-start | bytes 294920 | tf_op jit(solution)/shard_map/ppermute | solution.py:41
  16.6 9.2 %collective-permute-start.6 = (bf16[4,96,128]{2,1,0:T(8,128)(2,1)S(1)}, bf16[4,96,128]{2,1,0:T(8,128)(2,1)S(1)}, u32[]{:S(2)}, u32[]{:S(2)}) collective-permute-start(bf16[4,96,128]{2,1,0:T(8,128)(2,1)S(1)} %get-tuple-element.34.after), channel_id=1, source_target_pairs={{1,2},{2,1},{3,4},{4,3},{5,6},{6,5},{7,8},{8,7},{9,10},{10,9},{11,... | collective-permute-start | bytes 294920 | tf_op jit(solution)/shard_map/ppermute | solution.py:41
  28.4 11.0 %collective-permute-start.7 = (bf16[9,32,128]{2,1,0:T(8,128)(2,1)S(1)}, bf16[9,32,128]{2,1,0:T(8,128)(2,1)S(1)}, u32[]{:S(2)}, u32[]{:S(2)}) collective-permute-start(bf16[9,32,128]{2,1,0:T(8,128)(2,1)S(1)} %get-tuple-element.51), channel_id=1, source_target_pairs={{0,16},{16,0},{32,48},{48,32},{64,80},{80,64},{96,112},{112,96},{1... | collective-permute-start | bytes 221192 | tf_op jit(solution)/shard_map/ppermute | solution.py:41
  28.5 10.9 %collective-permute-start.8 = (bf16[9,32,128]{2,1,0:T(8,128)(2,1)S(1)}, bf16[9,32,128]{2,1,0:T(8,128)(2,1)S(1)}, u32[]{:S(2)}, u32[]{:S(2)}) collective-permute-start(bf16[9,32,128]{2,1,0:T(8,128)(2,1)S(1)} %get-tuple-element.52), channel_id=1, source_target_pairs={{16,32},{32,16},{48,64},{64,48},{80,96},{96,80},{112,128},{128,112... | collective-permute-start | bytes 221192 | tf_op jit(solution)/shard_map/ppermute | solution.py:41
  31.7 7.7 %collective-permute-start.9 = (bf16[9,32,128]{2,1,0:T(8,128)(2,1)S(1)}, bf16[9,32,128]{2,1,0:T(8,128)(2,1)S(1)}, u32[]{:S(2)}, u32[]{:S(2)}) collective-permute-start(bf16[9,32,128]{2,1,0:T(8,128)(2,1)S(1)} %get-tuple-element.53), channel_id=1, source_target_pairs={{0,1},{1,0},{2,3},{3,2},{4,5},{5,4},{6,7},{7,6},{8,9},{9,8},{10,11... | collective-permute-start | bytes 221192 | tf_op jit(solution)/shard_map/ppermute | solution.py:41
  32.7 8.0 %collective-permute-start.10 = (bf16[9,32,128]{2,1,0:T(8,128)(2,1)S(1)}, bf16[9,32,128]{2,1,0:T(8,128)(2,1)S(1)}, u32[]{:S(2)}, u32[]{:S(2)}) collective-permute-start(bf16[9,32,128]{2,1,0:T(8,128)(2,1)S(1)} %get-tuple-element.54), channel_id=1, source_target_pairs={{1,2},{2,1},{3,4},{4,3},{5,6},{6,5},{7,8},{8,7},{9,10},{10,9},{11,... | collective-permute-start | bytes 221192 | tf_op jit(solution)/shard_map/ppermute | solution.py:41

commit v4 on v3

--- a/solution.py
+++ b/solution.py
@@ -52,7 +52,11 @@
 
 def fetch(*refs):
     count = (len(refs) - 1) // 2
-    copies = [pltpu.make_async_copy(refs[n], refs[count + n], refs[-1].at[n]) for n in range(count)]
+    sems = refs[-1]
+    copies = [
+        pltpu.make_async_copy(refs[0].at[pl.ds(2 * n, 2)], refs[count].at[pl.ds(2 * n, 2)], sems.at[n]) for n in range(8)
+    ]
+    copies += [pltpu.make_async_copy(refs[n], refs[count + n], sems.at[7 + n]) for n in range(1, count)]
     for copy in copies:
         copy.start()
     for copy in copies:
@@ -208,15 +212,20 @@
     out[...] = sum0[part] + sum1[part] + sum2[part]
 
 
-def finish(own, r0, r1, r2, r3, out):
-    for c in range(OWN):
+def finish(own, r0, r1, r2, r3, out, built, sems):
+    copies = []
+    for c in (1, 0):
         for s in range(KC):
             value = own[c * KC + s]
             if c == 0:
                 for r in (r0, r1, r2, r3):
                     value = value + r[s].astype(F32)
-            out[c, 0:HALF, s * 64 : (s + 1) * 64] = value[:, 0:64]
-            out[c, HALF:64, s * 64 : (s + 1) * 64] = value[:, 64:128]
+            built[c, 0:HALF, s * 64 : (s + 1) * 64] = value[:, 0:64]
+            built[c, HALF:64, s * 64 : (s + 1) * 64] = value[:, 64:128]
+        copies.append(pltpu.make_async_copy(built.at[c], out.at[c], sems.at[c]))
+        copies[-1].start()
+    for copy in copies:
+        copy.wait()
 
 
 def shards(a_blocks, p_blocks, a_slot, halo_rows, p_cols, t_slot):
@@ -231,7 +240,7 @@
     sources = [p_blocks, halo_rows, a_slot.T, p_cols.T, t_slot.transpose(1, 3, 2, 0)]
     held, wanted, a_slot, p_cols, t_slot = pl.pallas_call(
         fetch, out_shape=[jax.ShapeDtypeStruct(x.shape, x.dtype) for x in sources],
-        in_specs=[HBM] * 5, out_specs=[VMEM] * 5, scratch_shapes=[pltpu.SemaphoreType.DMA((5,))],
+        in_specs=[HBM] * 5, out_specs=[VMEM] * 5, scratch_shapes=[pltpu.SemaphoreType.DMA((12,))],
         compiler_params=params(2), cost_estimate=cost(0, 800000), name="fetch",
     )(*[pltpu.with_memory_space_constraint(x, pltpu.HBM) for x in sources])
     piece = jax.ShapeDtypeStruct((4, 96, 128), BF16)
@@ -282,7 +291,8 @@
     return pl.pallas_call(
         finish,
         out_shape=jax.ShapeDtypeStruct((OWN, 64, KC * 64), F32),
-        in_specs=[VMEM] * 5, out_specs=VMEM,
+        in_specs=[VMEM] * 5, out_specs=HBM,
+        scratch_shapes=[pltpu.VMEM((OWN, 64, KC * 64), F32), pltpu.SemaphoreType.DMA((OWN,))],
         compiler_params=params(4), cost_estimate=cost(0, 1000000), name="finish",
     )(own, *got)
 

time: 41.7 us -> 41.7 us (level)
  no operation moved by 1% of the time
where the time goes in v4:
time: 41.7 us; the launch traced here: 41.6 us
  starting transfers between devices  22.3 us (53%)
  Pallas kernels  13.7 us (33%)
  waiting for transfers between devices  5.35 us (13%)
    ppermute x11, starting transfers between devices, swapped(): return lax.ppermute(value, axis, pairs)  22.3 us
    ppermute x11, waiting for transfers between devices, swapped(): return lax.ppermute(value, axis, pairs)  5.35 us
    pallas_call x1, Pallas kernels, shards(): pl.pallas_call(early, out_shape=[LEFT, RIGHT] + SUMS + [jax.ShapeDtypeStr...  5.24 us
    pallas_call x1, Pallas kernels, shards(): pl.pallas_call(inward, out_shape=[jax.ShapeDtypeStruct((OWN * KC, HALF, 1...  3.22 us
    pallas_call x1, Pallas kernels, shards(): pl.pallas_call(outward, out_shape=[packed] * 4 + [RIGHT] + SUMS, in_specs...  2.48 us
    pallas_call x1, Pallas kernels, shards(): pl.pallas_call(fetch, out_shape=[jax.ShapeDtypeStruct(x.shape, x.dtype) f...  1.17 us
    pallas_call x1, Pallas kernels, shards(): pl.pallas_call(finish, out_shape=jax.ShapeDtypeStruct((OWN, 64, KC * 64),...  0.84 us
  transfers between devices with their start and end apart: 11, of which 3 were waited for; matrix products, arithmetic and copies ran while one was open for 0% of the time, Pallas kernels for 25%

profile of v4, /device:TPU:0, one launch (start us, length us, event | category | flops | bytes accessed | tf_op | source)
XLA Modules:
  0.0 41.6 jit_solution(7993111876582694673)
XLA Ops:
  0.0 0.0 collective-permute-start
  0.0 2.3 %collective-permute-start.1 = (s32[1,4,4]{2,1,0:T(4,128)}, s32[1,4,4]{2,1,0:T(4,128)S(1)}, u32[]{:S(2)}, u32[]{:S(2)}) collective-permute-start(s32[1,4,4]{2,1,0:T(4,128)} %refs_1_.1), channel_id=1, source_target_pairs={{16,32},{32,16},{48,64},{64,48},{80,96},{96,80},{112,128},{128,112... | collective-permute-start | bytes 200 | tf_op jit(solution)/shard_map/ppermute | solution.py:41
  2.4 8.0 %collective-permute-start.3 = (s32[1,4,4]{2,1,0:T(4,128)}, s32[1,4,4]{2,1,0:T(4,128)S(1)}, u32[]{:S(2)}, u32[]{:S(2)}) collective-permute-start(s32[1,4,4]{2,1,0:T(4,128)} %refs_1_.1), channel_id=1, source_target_pairs={{1,2},{2,1},{3,4},{4,3},{5,6},{6,5},{7,8},{8,7},{9,10},{10,9},{11,... | collective-permute-start | bytes 200 | tf_op jit(solution)/shard_map/ppermute | solution.py:41
  10.4 0.0 collective-permute-start.2
  10.4 0.1 pad_add_fusion.sides
  10.5 1.2 %fetch.1 = (bf16[16,64,192]{2,1,0:T(8,128)(2,1)S(1)}, s32[1,4,4]{2,1,0:T(4,128)S(1)}, s32[7,16]{1,0:T(8,128)S(1)}, s32[3,16]{1,0:T(4,128)S(1)}, s32[3,3,7,16]{3,2,1,0:T(8,128)S(1)}) custom-call(bf16[16,64,192]{2,1,0:T(8,128)(2,1)} %refs_0_.1, s32[1,4,4]{2,1,0:T(4,128)} %refs_1_.1, s32[7,16]{1,0:T(8,128)} %bitcast.6, s32[3,16]{1,0:T(4,128)} %bitcast.7, ...), custom_call_target="tpu_custom_call" | custom-call | bytes 800000 | tf_op jit(solution)/shard_map/fetch/pallas_call | solution.py:241
  11.6 0.0 collective-permute-done.1.cross
  11.6 0.5 %collective-permute-done.3.far = s32[1,4,4]{2,1,0:T(4,128)S(1)} collective-permute-done((s32[1,4,4]{2,1,0:T(4,128)}, s32[1,4,4]{2,1,0:T(4,128)S(1)}, u32[]{:S(2)}, u32[]{:S(2)}) %collective-permute-start.3) | collective-permute-done | bytes 96 | tf_op jit(solution)/shard_map/ppermute | solution.py:41
  12.2 3.5 %collective-permute-done.2.near = s32[1,4,4]{2,1,0:T(4,128)S(1)} collective-permute-done((s32[1,4,4]{2,1,0:T(4,128)}, s32[1,4,4]{2,1,0:T(4,128)S(1)}, u32[]{:S(2)}, u32[]{:S(2)}) %collective-permute-start.2) | collective-permute-done | bytes 96 | tf_op jit(solution)/shard_map/ppermute | solution.py:41
  15.7 0.7 %gather_rows.1 = (bf16[4,96,128]{2,1,0:T(8,128)(2,1)S(1)}, bf16[4,96,128]{2,1,0:T(8,128)(2,1)S(1)}, bf16[4,96,128]{2,1,0:T(8,128)(2,1)S(1)}) custom-call(s32[2]{0:T(128)S(1)} %pad_add_fusion.sides, s32[1,4,4]{2,1,0:T(4,128)S(1)} %collective-permute-done.1.cross, s32[1,4,4]{2,1,0:T(4,128)S(1)} %collective-permute-done.2.near, ...), custom_call_target="tpu_custom_call" | custom-call | bytes 700000 | tf_op jit(solution)/shard_map/gather_rows/pallas_call | solution.py:247
  16.4 0.1 collective-permute-start.4
  16.5 0.1 collective-permute-start.5
  16.6 3.9 %collective-permute-start.6 = (bf16[4,96,128]{2,1,0:T(8,128)(2,1)S(1)}, bf16[4,96,128]{2,1,0:T(8,128)(2,1)S(1)}, u32[]{:S(2)}, u32[]{:S(2)}) collective-permute-start(bf16[4,96,128]{2,1,0:T(8,128)(2,1)S(1)} %get-tuple-element.34.after), channel_id=1, source_target_pairs={{1,2},{2,1},{3,4},{4,3},{5,6},{6,5},{7,8},{8,7},{9,10},{10,9},{11,... | collective-permute-start | bytes 294920 | tf_op jit(solution)/shard_map/ppermute | solution.py:41
  20.6 0.0 collective-permute-done.chip
  20.6 5.2 %early.1 = (bf16[112,96,128]{2,1,0:T(8,128)(2,1)S(1)}, bf16[32,3,128,128]{3,2,1,0:T(8,128)(2,1)S(1)}, f32[54,32,128]{2,1,0:T(8,128)S(1)}, f32[54,32,128]{2,1,0:T...) custom-call(s32[2]{0:T(128)S(1)} %pad_add_fusion.sides, ...), custom_call_target="tpu_custom_call" | custom-call | flops 400000000 | bytes 6000000 | tf_op jit(solution)/shard_map/early/pallas_call | solution.py:255
  25.8 0.0 collective-permute-done.4.cross
  25.8 0.0 collective-permute-done.5.near
  25.9 0.0 collective-permute-done.6.far
  25.9 2.5 %outward.1 = (bf16[9,32,128]{2,1,0:T(8,128)(2,1)S(1)}, bf16[9,32,128]{2,1,0:T(8,128)(2,1)S(1)}, bf16[9,32,128]{2,1,0:T(8,128)(2,1)S(1)}, bf16[9,32,128]{2,1,0:T(...) custom-call(s32[3,3,7,16]{3,2,1,0:T(8,128)S(1)} %get-tuple-element.3, ...), custom_call_target="tpu_custom_call", output_to_operand_aliasing={{4}: (4, {}), {5}: (5, {}), {6}: (6, {}), {7}: (7, {})} | custom-call | flops 400000000 | bytes 6000000 | tf_op jit(solution)/shard_map/outward/pallas_call | solution.py:271
  28.4 0.1 collective-permute-start.7
  28.5 3.3 %collective-permute-start.8 = (bf16[9,32,128]{2,1,0:T(8,128)(2,1)S(1)}, bf16[9,32,128]{2,1,0:T(8,128)(2,1)S(1)}, u32[]{:S(2)}, u32[]{:S(2)}) collective-permute-start(bf16[9,32,128]{2,1,0:T(8,128)(2,1)S(1)} %get-tuple-element.52), channel_id=1, source_target_pairs={{16,32},{32,16},{48,64},{64,48},{80,96},{96,80},{112,128},{128,112... | collective-permute-start | bytes 221192 | tf_op jit(solution)/shard_map/ppermute | solution.py:41
  31.7 1.0 %collective-permute-start.9 = (bf16[9,32,128]{2,1,0:T(8,128)(2,1)S(1)}, bf16[9,32,128]{2,1,0:T(8,128)(2,1)S(1)}, u32[]{:S(2)}, u32[]{:S(2)}) collective-permute-start(bf16[9,32,128]{2,1,0:T(8,128)(2,1)S(1)} %get-tuple-element.53), channel_id=1, source_target_pairs={{0,1},{1,0},{2,3},{3,2},{4,5},{5,4},{6,7},{7,6},{8,9},{9,8},{10,11... | collective-permute-start | bytes 221192 | tf_op jit(solution)/shard_map/ppermute | solution.py:41
  32.7 3.4 %collective-permute-start.10 = (bf16[9,32,128]{2,1,0:T(8,128)(2,1)S(1)}, bf16[9,32,128]{2,1,0:T(8,128)(2,1)S(1)}, u32[]{:S(2)}, u32[]{:S(2)}) collective-permute-start(bf16[9,32,128]{2,1,0:T(8,128)(2,1)S(1)} %get-tuple-element.54), channel_id=1, source_target_pairs={{1,2},{2,1},{3,4},{4,3},{5,6},{6,5},{7,8},{8,7},{9,10},{10,9},{11,... | collective-permute-start | bytes 221192 | tf_op jit(solution)/shard_map/ppermute | solution.py:41
  36.2 3.2 %inward.1 = (f32[18,32,128]{2,1,0:T(8,128)S(1)}, f32[54,32,128]{2,1,0:T(8,128)S(1)}, f32[54,32,128]{2,1,0:T(8,128)S(1)}, f32[54,32,128]{2,1,0:T(8,128)S(1)}) custom-call(s32[3,3,7,16]{3,2,1,0:T(8,128)S(1)} %get-tuple-element.36.bins, s32[7,16]{1,0:T(8,128)S(1)} %get-tuple-element.37.slots, ...), custom_call_target="tpu_custom_call", output_to_operand_aliasing={{1}: (5, {}), {2}: (6, {}), {3}: (7, {})} | custom-call | flops 1000000000 | bytes 8000000 | tf_op jit(solution)/shard_map/inward/pallas_call | solution.py:283
  39.4 0.0 collective-permute-done.7.r0
  39.4 0.0 collective-permute-done.8.r1
  39.4 0.0 collective-permute-done.9.r2
  39.4 1.3 %collective-permute-done.10.r3 = bf16[9,32,128]{2,1,0:T(8,128)(2,1)S(1)} collective-permute-done((bf16[9,32,128]{2,1,0:T(8,128)(2,1)S(1)}, bf16[9,32,128]{2,1,0:T(8,128)(2,1)S(1)}, u32[]{:S(2)}, u32[]{:S(2)}) %collective-permute-start.10) | collective-permute-done | bytes 73760 | tf_op jit(solution)/shard_map/ppermute | solution.py:41
  40.7 0.8 %finish.1 = f32[2,64,576]{2,1,0:T(8,128)} custom-call(f32[18,32,128]{2,1,0:T(8,128)S(1)} %get-tuple-element.50.own, bf16[9,32,128]{2,1,0:T(8,128)(2,1)S(1)} %collective-permute-done.7.r0, bf16[9,32,128]{2,1,0:T(8,128)(2,1)S(1)} %collective-permute-done.8.r1, bf16[9,32,128]{2,1,0:T(8,128)(2,1)S(1)} %collective-permute-done.9.r2, ...), custom_call_target="tpu_custom_call" | custom-call | bytes 1000000 | tf_op jit(solution)/shard_map/finish/pallas_call | solution.py:291
Async XLA Ops:
  0.0 20.6 %collective-permute-start = (bf16[16,64,192]{2,1,0:T(8,128)(2,1)}, bf16[16,64,192]{2,1,0:T(8,128)(2,1)S(1)}, u32[]{:S(2)}, u32[]{:S(2)}) collective-permute-start(bf16[16,64,192]{2,1,0:T(8,128)(2,1)} %refs_0_.1), channel_id=1, source_target_pairs={{0,16},{16,0},{32,48},{48,32},{64,80},{80,64},{96,112},{112,96},{1... | collective-permute-start | bytes 1179656 | tf_op jit(solution)/shard_map/ppermute | solution.py:41
  0.0 11.6 %collective-permute-start.1 = (s32[1,4,4]{2,1,0:T(4,128)}, s32[1,4,4]{2,1,0:T(4,128)S(1)}, u32[]{:S(2)}, u32[]{:S(2)}) collective-permute-start(s32[1,4,4]{2,1,0:T(4,128)} %refs_1_.1), channel_id=1, source_target_pairs={{16,32},{32,16},{48,64},{64,48},{80,96},{96,80},{112,128},{128,112... | collective-permute-start | bytes 200 | tf_op jit(solution)/shard_map/ppermute | solution.py:41
  2.4 9.8 %collective-permute-start.3 = (s32[1,4,4]{2,1,0:T(4,128)}, s32[1,4,4]{2,1,0:T(4,128)S(1)}, u32[]{:S(2)}, u32[]{:S(2)}) collective-permute-start(s32[1,4,4]{2,1,0:T(4,128)} %refs_1_.1), channel_id=1, source_target_pairs={{1,2},{2,1},{3,4},{4,3},{5,6},{6,5},{7,8},{8,7},{9,10},{10,9},{11,... | collective-permute-start | bytes 200 | tf_op jit(solution)/shard_map/ppermute | solution.py:41
  10.4 5.3 %collective-permute-start.2 = (s32[1,4,4]{2,1,0:T(4,128)}, s32[1,4,4]{2,1,0:T(4,128)S(1)}, u32[]{:S(2)}, u32[]{:S(2)}) collective-permute-start(s32[1,4,4]{2,1,0:T(4,128)} %refs_1_.1), channel_id=1, source_target_pairs={{0,1},{1,0},{2,3},{3,2},{4,5},{5,4},{6,7},{7,6},{8,9},{9,8},{10,11... | collective-permute-start | bytes 200 | tf_op jit(solution)/shard_map/ppermute | solution.py:41
  16.4 9.4 %collective-permute-start.4 = (bf16[4,96,128]{2,1,0:T(8,128)(2,1)S(1)}, bf16[4,96,128]{2,1,0:T(8,128)(2,1)S(1)}, u32[]{:S(2)}, u32[]{:S(2)}) collective-permute-start(bf16[4,96,128]{2,1,0:T(8,128)(2,1)S(1)} %get-tuple-element.44), channel_id=1, source_target_pairs={{16,32},{32,16},{48,64},{64,48},{80,96},{96,80},{112,128},{128,112... | collective-permute-start | bytes 294920 | tf_op jit(solution)/shard_map/ppermute | solution.py:41
  16.5 9.3 %collective-permute-start.5 = (bf16[4,96,128]{2,1,0:T(8,128)(2,1)S(1)}, bf16[4,96,128]{2,1,0:T(8,128)(2,1)S(1)}, u32[]{:S(2)}, u32[]{:S(2)}) collective-permute-start(bf16[4,96,128]{2,1,0:T(8,128)(2,1)S(1)} %get-tuple-element.45), channel_id=1, source_target_pairs={{0,1},{1,0},{2,3},{3,2},{4,5},{5,4},{6,7},{7,6},{8,9},{9,8},{10,11... | collective-permute-start | bytes 294920 | tf_op jit(solution)/shard_map/ppermute | solution.py:41
  16.6 9.2 %collective-permute-start.6 = (bf16[4,96,128]{2,1,0:T(8,128)(2,1)S(1)}, bf16[4,96,128]{2,1,0:T(8,128)(2,1)S(1)}, u32[]{:S(2)}, u32[]{:S(2)}) collective-permute-start(bf16[4,96,128]{2,1,0:T(8,128)(2,1)S(1)} %get-tuple-element.34.after), channel_id=1, source_target_pairs={{1,2},{2,1},{3,4},{4,3},{5,6},{6,5},{7,8},{8,7},{9,10},{10,9},{11,... | collective-permute-start | bytes 294920 | tf_op jit(solution)/shard_map/ppermute | solution.py:41
  28.4 11.0 %collective-permute-start.7 = (bf16[9,32,128]{2,1,0:T(8,128)(2,1)S(1)}, bf16[9,32,128]{2,1,0:T(8,128)(2,1)S(1)}, u32[]{:S(2)}, u32[]{:S(2)}) collective-permute-start(bf16[9,32,128]{2,1,0:T(8,128)(2,1)S(1)} %get-tuple-element.51), channel_id=1, source_target_pairs={{0,16},{16,0},{32,48},{48,32},{64,80},{80,64},{96,112},{112,96},{1... | collective-permute-start | bytes 221192 | tf_op jit(solution)/shard_map/ppermute | solution.py:41
  28.5 10.9 %collective-permute-start.8 = (bf16[9,32,128]{2,1,0:T(8,128)(2,1)S(1)}, bf16[9,32,128]{2,1,0:T(8,128)(2,1)S(1)}, u32[]{:S(2)}, u32[]{:S(2)}) collective-permute-start(bf16[9,32,128]{2,1,0:T(8,128)(2,1)S(1)} %get-tuple-element.52), channel_id=1, source_target_pairs={{16,32},{32,16},{48,64},{64,48},{80,96},{96,80},{112,128},{128,112... | collective-permute-start | bytes 221192 | tf_op jit(solution)/shard_map/ppermute | solution.py:41
  31.7 7.7 %collective-permute-start.9 = (bf16[9,32,128]{2,1,0:T(8,128)(2,1)S(1)}, bf16[9,32,128]{2,1,0:T(8,128)(2,1)S(1)}, u32[]{:S(2)}, u32[]{:S(2)}) collective-permute-start(bf16[9,32,128]{2,1,0:T(8,128)(2,1)S(1)} %get-tuple-element.53), channel_id=1, source_target_pairs={{0,1},{1,0},{2,3},{3,2},{4,5},{5,4},{6,7},{7,6},{8,9},{9,8},{10,11... | collective-permute-start | bytes 221192 | tf_op jit(solution)/shard_map/ppermute | solution.py:41
  32.7 8.0 %collective-permute-start.10 = (bf16[9,32,128]{2,1,0:T(8,128)(2,1)S(1)}, bf16[9,32,128]{2,1,0:T(8,128)(2,1)S(1)}, u32[]{:S(2)}, u32[]{:S(2)}) collective-permute-start(bf16[9,32,128]{2,1,0:T(8,128)(2,1)S(1)} %get-tuple-element.54), channel_id=1, source_target_pairs={{1,2},{2,1},{3,4},{4,3},{5,6},{6,5},{7,8},{8,7},{9,10},{10,9},{11,... | collective-permute-start | bytes 221192 | tf_op jit(solution)/shard_map/ppermute | solution.py:41
